TPU v7x, 32 devices: a whole 2x2x4 slice. The times are simulated.
32 devices in a mesh: pts: 8 (over z, core), head: 4 (over y, x).
Axes of the slice: x: 2, y: 2, z: 4, core: 2. Of those that a mesh axis runs over, the one named last changes fastest.
Arguments:
- mesh_signals: bfloat16 [262144, 256], P('pts'), may hold values from -7 to 7
- loss_sensitivity: bfloat16 [262144, 256], P(('pts', 'head')), may hold values from -0.01171875 to 0.01171875
- divider_projection: bfloat16 [256, 256], P(None, 'head'), may hold values from -0.375 to 0.375
- partition_projection: bfloat16 [256, 256], P(None, 'head'), may hold values from -0.375 to 0.375
- sharpness_axis: float32 [256], P('head'), may hold values from -4 to 4
- partition_energies: float32 [8, 32, 64], P('head'), may hold values from -6 to 6
- asking_projection: float32 [8, 32, 32], P('head'), may hold values from -6 to 6
- lookup_projection: float32 [8, 32, 32], P('head'), may hold values from -6 to 6
- content_projection: float32 [8, 32, 32], P('head'), may hold values from -1 to 1
- prefocus_scale: float32 [256], replicated, may hold values from 0.1 to 1.9
- emit_projection: bfloat16 [256, 256], replicated, may hold values from -0.375 to 0.375
- premlp_scale: float32 [256], replicated, may hold values from 0.1 to 1.9
- expand_factor: bfloat16 [256, 256], replicated, may hold values from -0.375 to 0.375
- expand_offset: float32 [256], replicated, may hold values from -3 to 3
- contract_factor: bfloat16 [256, 256], replicated, may hold values from -0.375 to 0.375
Outputs:
- block_result: bfloat16 [262144, 256], P(('pts', 'head'))
- divider_proj_slope: float32 [256, 256], P(None, 'head')
- partition_proj_slope: float32 [256, 256], P(None, 'head')
- sharpness_axis_slope: float32 [256], P('head')
- partition_energy_slope: float32 [8, 32, 64], P('head')
- asking_proj_slope: float32 [8, 32, 32], P('head')
- lookup_proj_slope: float32 [8, 32, 32], P('head')
- content_proj_slope: float32 [8, 32, 32], P('head')
- prefocus_scale_slope: float32 [256], replicated
- emit_proj_slope: float32 [256, 256], replicated
- premlp_scale_slope: float32 [256], replicated
- expand_factor_slope: float32 [256, 256], replicated
- expand_offset_slope: float32 [256], replicated
- contract_factor_slope: float32 [256, 256], replicated
All inputs are finite; a program needn't handle non-finite values.
Results may differ from a plain program's by a relative error of at most 0.011.
Values may be sent and summed in bfloat16 or wider, within the bound.
No kernel may reach another device: no remote copies, remote signals or barrier semaphores. Data moves between devices by JAX's collectives and lax.ppermute only.
A program may use at most 256 MiB of HBM per device.

v0:
```python
import functools

import jax
import jax.numpy as jnp
from jax import lax
from jax.experimental import pallas as pl
from jax.experimental.pallas import tpu as pltpu
from jax.sharding import PartitionSpec as P


SCORE_LIMIT = 30.0
NORM_EPS = 1e-05
GELU_SCALE = 0.7978845608028654
GELU_CUBE = 0.044715
HIGHEST = lax.Precision.HIGHEST
PAD = 16


NN = (((1,), (0,)), ((), ()))
NT = (((1,), (1,)), ((), ()))
TN = (((0,), (0,)), ((), ()))


def dot(a, b, numbers=NN, precision=None):
    return lax.dot_general(a, b, numbers, precision=precision, preferred_element_type=jnp.float32)


def axis_groups(axis):
    size = lax.axis_size(axis)
    groups = []
    stride = 1
    step = 2 if axis == "pts" else 4
    while stride < size:
        count = min(step, size // stride)
        groups.append((axis, stride, count))
        stride *= count
        step = 4
    return groups


def swap(value, axis, distance):
    size = lax.axis_size(axis)
    return lax.ppermute(value, axis, [(i, i ^ distance) for i in range(size)])


def tree_sum(parts):
    while len(parts) > 1:
        parts = [parts[i] + parts[i + 1] for i in range(0, len(parts), 2)]
    return parts[0]


def group_sum(value, group):
    axis, stride, count = group
    return tree_sum([value] + [swap(value, axis, m * stride) for m in range(1, count)])


def all_sum(value, groups):
    for group in groups:
        value = group_sum(value, group)
    return value


def exchange_sum(value, axes):
    count = 1
    for axis in axes:
        count *= lax.axis_size(axis)
    block = value.shape[0] // count
    pieces = lax.all_to_all(value.reshape(count, block, value.shape[1]), axes, 0, 0, tiled=True)
    return jnp.sum(pieces.astype(jnp.float32), axis=0)


def gather(value, axes):
    count = 1
    for axis in axes:
        count *= lax.axis_size(axis)
    full = lax.all_to_all(
        jnp.broadcast_to(value[None], (count,) + value.shape), axes, 0, 0, tiled=True
    )
    return full.reshape((count * value.shape[0],) + value.shape[1:])


def same_head(shape, row_span, column_span):
    rows = lax.broadcasted_iota(jnp.int32, shape, 0) // row_span
    columns = lax.broadcasted_iota(jnp.int32, shape, 1) // column_span
    return rows == columns


def fold_heads(full, heads, width, slices):
    kept = jnp.where(same_head(full.shape, width, slices), full, 0.0)
    return jnp.sum(kept.reshape(heads, width, heads * slices), axis=0)


def sharp_terms(raw):
    sharpness = 0.5 + jnp.maximum(raw, 0.0) + jnp.log1p(jnp.exp(-jnp.abs(raw)))
    return 1.0 / sharpness


def spread_column(row):
    count = row.shape[1]
    square = jnp.broadcast_to(row, (count, count))
    return jnp.sum(jnp.where(same_head((count, count), 1, 1), square, 0.0), axis=1, keepdims=True)


def pack_kernel(div_ref, part_ref, sharp_ref, energy_ref, ask_ref, look_ref, content_ref, out_ref):
    local, channels, slices = energy_ref.shape
    copies, _, width = out_ref.shape
    div = div_ref[...].astype(jnp.float32)
    part = part_ref[...].astype(jnp.float32)
    for h in range(local):
        base = 3 * channels * h
        own = slice(h * channels, (h + 1) * channels)
        sharp = spread_column(sharp_ref[0:1, own])
        rest = jnp.concatenate(
            [
                energy_ref[h],
                ask_ref[h],
                look_ref[h],
                content_ref[h],
                jnp.broadcast_to(sharp, (channels, width - slices - 3 * channels)),
            ],
            axis=1,
        )
        for g in range(copies):
            out_ref[g, base : base + channels, :] = div[own]
            out_ref[g, base + channels : base + 2 * channels, :] = part[own]
            out_ref[g, base + 2 * channels : base + 3 * channels, :] = rest


def unpack_kernel(
    all_ref, high_ref, low_ref, energy_ref, div_ref, part_ref, ask_ref, look_ref, content_ref
):
    heads, channels, _ = ask_ref.shape
    lanes = high_ref.shape[0] - PAD
    slices = lanes // heads
    energy_ref[...] = jnp.zeros_like(energy_ref)
    for h in range(heads):
        base = 3 * channels * h
        own = slice(h * channels, (h + 1) * channels)
        div_ref[own, :] = all_ref[base : base + channels, :].astype(jnp.bfloat16)
        part_ref[own, :] = all_ref[base + channels : base + 2 * channels, :].astype(jnp.bfloat16)
        rest = all_ref[base + 2 * channels : base + 3 * channels, :]
        energy_ref[own, h * slices : (h + 1) * slices] = rest[:, :slices]
        ask_ref[h] = rest[:, slices : slices + channels]
        look_ref[h] = rest[:, slices + channels : slices + 2 * channels]
        content_ref[h] = rest[:, slices + 2 * channels : slices + 3 * channels]
        spot = slices + 3 * channels
        energy_ref[own, lanes + h : lanes + h + 1] = rest[:, spot : spot + 1]
    logits_of = dot(energy_ref[...], div_ref[...].astype(jnp.float32), TN, HIGHEST)
    high = logits_of.astype(jnp.bfloat16)
    high_ref[...] = high
    low_ref[...] = (logits_of - high.astype(jnp.float32)).astype(jnp.bfloat16)


def finish_kernel(
    in_ref, div_ref, part_ref, energy_ref, sharp_ref, scale_ref, premlp_ref, offset_ref
):
    local, channels, slices = energy_ref.shape
    unit = 2 * channels + 16
    div = []
    part = []
    for h in range(local):
        base = h * unit
        div.append(in_ref[base : base + channels, :])
        part.append(in_ref[base + channels : base + 2 * channels, :])
        tail = in_ref[base + 2 * channels : base + unit, :]
        tail = jnp.concatenate([tail[:, :128], tail[:, 128:]], axis=0)
        energy_ref[h] = tail[:, :slices]
        square = tail[:, slices : slices + channels]
        kept = jnp.where(same_head((channels, channels), 1, 1), square, 0.0)
        sharp_ref[0:1, h * channels : (h + 1) * channels] = jnp.sum(kept, axis=0, keepdims=True)
    div_ref[...] = jnp.concatenate(div, axis=0)
    part_ref[...] = jnp.concatenate(part, axis=0)
    base = local * unit
    scale_ref[...] = in_ref[base : base + 1, :]
    premlp_ref[...] = in_ref[base + 1 : base + 2, :]
    offset_ref[...] = in_ref[base + 2 : base + 3, :]


def norm_kernel(member_ref, x_ref, gain_ref, s_ref):
    x = x_ref[...].astype(jnp.float32)
    centered = x - jnp.mean(x, axis=1, keepdims=True)
    spread = jnp.mean(centered * centered, axis=1, keepdims=True)
    scaled = centered * lax.rsqrt(spread + NORM_EPS) * gain_ref[...]
    s_ref[...] = scaled.astype(jnp.bfloat16)


def front_kernel(
    s_ref,
    high_ref,
    low_ref,
    feat_ref,
    w_ref,
    m_ref,
    tot_ref,
    z_scr,
    r_scr,
    den_scr,
    *,
    heads,
    slices,
    chunk,
):
    step = pl.program_id(0)
    lanes = heads * slices

    @pl.when(step == 0)
    def _():
        m_ref[...] = jnp.zeros_like(m_ref)
        den_scr[...] = jnp.zeros_like(den_scr)

    scaled = s_ref[...]
    z_scr[...] = dot(high_ref[...], scaled, NT) + dot(low_ref[...], scaled, NT)
    r_scr[...] = sharp_terms(z_scr[lanes : lanes + heads, :]) * (1.0 / SCORE_LIMIT)
    rows = s_ref.shape[0]
    for h in range(heads):
        span = slice(h * slices, (h + 1) * slices)
        for c in range(rows // chunk):
            cols = slice(c * chunk, (c + 1) * chunk)
            z = z_scr[span, cols] * r_scr[h : h + 1, cols]
            raised = jnp.exp(SCORE_LIMIT * jnp.tanh(z))
            weights = raised * (1.0 / jnp.sum(raised, axis=0, keepdims=True))
            w_ref[span, cols] = weights.astype(jnp.bfloat16)
            part = weights[:, 0:128]
            for k in range(1, chunk // 128):
                part = part + weights[:, k * 128 : (k + 1) * 128]
            den_scr[span, :] += part
    m_ref[...] += dot(w_ref[...], scaled)

    @pl.when(step == pl.num_programs(0) - 1)
    def _():
        full = dot(feat_ref[...].astype(jnp.float32), m_ref[...], NT, HIGHEST)
        width = full.shape[0] // heads
        tot_ref[0:width, :] = fold_heads(full, heads, width, slices)
        ones = jnp.ones((8, 128), jnp.float32)
        tot_ref[width : width + 8, :] = dot(ones, den_scr[...], NT, HIGHEST)


def mixer_kernel(
    member_ref,
    x_ref,
    w_ref,
    loss_ref,
    te_ref,
    gain_ref,
    expand_ref,
    expand_t_ref,
    offset_ref,
    contract_ref,
    contract_t_ref,
    token_ref,
    emit_ref,
    block_ref,
    back_ref,
    grads_ref,
    gains_ref,
    tg_ref,
    acc_scr,
    wr_scr,
    gain_scr,
    *,
    heads,
    slices,
):
    step = pl.program_id(0)
    width = emit_ref.shape[0]

    @pl.when(step == 0)
    def _():
        acc_scr[...] = jnp.zeros_like(acc_scr)
        gain_scr[...] = jnp.zeros_like(gain_scr)
        wr_scr[...] = jnp.zeros_like(wr_scr)

    weights = w_ref[...]
    loss = loss_ref[...]
    residual = x_ref[...].astype(jnp.float32) + dot(weights, te_ref[...], TN)
    centered = residual - jnp.mean(residual, axis=1, keepdims=True)
    spread = jnp.mean(centered * centered, axis=1, keepdims=True)
    rstd = lax.rsqrt(spread + NORM_EPS)
    normal = centered * rstd
    gain = gain_ref[...]
    normed = (normal * gain).astype(jnp.bfloat16)
    inner = dot(normed, expand_ref[...]) + offset_ref[...]
    square = inner * inner
    bent = jnp.tanh(GELU_SCALE * inner * (1.0 + GELU_CUBE * square))
    half = 0.5 * (1.0 + bent)
    active = (inner * half).astype(jnp.bfloat16)
    slope = half + 0.5 * inner * (1.0 - bent * bent) * (
        GELU_SCALE + (3.0 * GELU_CUBE * GELU_SCALE) * square
    )
    block_ref[...] = (residual + dot(active, contract_ref[...])).astype(jnp.bfloat16)
    back_inner = dot(loss, contract_t_ref[...]) * slope
    back_low = back_inner.astype(jnp.bfloat16)
    back_normed = dot(back_low, expand_t_ref[...])
    gained = back_normed * normal
    pulled = back_normed * gain
    mean_pull = jnp.mean(pulled, axis=1, keepdims=True)
    mean_gain = jnp.mean(pulled * normal, axis=1, keepdims=True)
    back_resid = loss.astype(jnp.float32) + rstd * (pulled - mean_pull - normal * mean_gain)
    back = back_resid.astype(jnp.bfloat16)
    back_ref[...] = back
    acc_scr[0:width, :] += dot(normed, back_low, TN)
    acc_scr[width : 2 * width, :] += dot(active, loss, TN)
    rows = x_ref.shape[0]
    gain_scr[0:8, :] += jnp.sum(gained.reshape(rows // 8, 8, width), axis=0)
    gain_scr[8:16, :] += jnp.sum(back_inner.reshape(rows // 8, 8, width), axis=0)
    wr_scr[...] += dot(weights, back)

    @pl.when(step == pl.num_programs(0) - 1)
    def _():
        grads_ref[0:width, :] = dot(
            token_ref[...].astype(jnp.float32), wr_scr[...], NN, HIGHEST
        ).astype(jnp.bfloat16)
        grads_ref[width : 3 * width, :] = acc_scr[...].astype(jnp.bfloat16)
        full = dot(emit_ref[...].astype(jnp.float32), wr_scr[...], NT, HIGHEST)
        tg_ref[...] = fold_heads(full, heads, full.shape[0] // heads, slices)
        gains_ref[...] = jnp.zeros_like(gains_ref)
        gains_ref[1:2, :] = jnp.sum(gain_scr[0:8, :], axis=0, keepdims=True)
        gains_ref[2:3, :] = jnp.sum(gain_scr[8:16, :], axis=0, keepdims=True)


def back_kernel(
    s_ref,
    back_ref,
    high_ref,
    low_ref,
    te_ref,
    fb_ref,
    den_ref,
    m_ref,
    energy_ref,
    num_ref,
    div_ref,
    part_ref,
    scale_ref,
    gains_ref,
    out_ref,
    z_scr,
    b_scr,
    r_scr,
    d_scr,
    g_scr,
    *,
    heads,
    slices,
    chunk,
    local,
    block,
):
    step = pl.program_id(0)
    lanes = heads * slices

    @pl.when(step == 0)
    def _():
        g_scr[...] = jnp.zeros_like(g_scr)
        d_scr[...] = jnp.zeros_like(d_scr)

    scaled = s_ref[...]
    z_scr[...] = dot(high_ref[...], scaled, NT) + dot(low_ref[...], scaled, NT)
    b_scr[...] = dot(te_ref[...], back_ref[...], NT) + dot(fb_ref[...], scaled, NT)
    raw = z_scr[lanes : lanes + heads, :]
    r_scr[...] = sharp_terms(raw)
    rows = s_ref.shape[0]
    for h in range(heads):
        span = slice(h * slices, (h + 1) * slices)
        for c in range(rows // chunk):
            cols = slice(c * chunk, (c + 1) * chunk)
            inverse = r_scr[h : h + 1, cols]
            z = z_scr[span, cols] * (inverse * (1.0 / SCORE_LIMIT))
            bent = jnp.tanh(z)
            raised = jnp.exp(SCORE_LIMIT * bent)
            weights = raised * (1.0 / jnp.sum(raised, axis=0, keepdims=True))
            back_w = b_scr[span, cols] + jnp.concatenate([den_ref[span, :]] * (chunk // 128), axis=1)
            middle = jnp.sum(weights * back_w, axis=0, keepdims=True)
            q = weights * (back_w - middle) * (1.0 - bent * bent)
            d_scr[span, cols] = (q * inverse).astype(jnp.bfloat16)
            z_scr[lanes + 8 + h : lanes + 9 + h, cols] = jnp.sum(q * z, axis=0, keepdims=True)
    pulled = z_scr[lanes + 8 : lanes + 8 + heads, :] * (-SCORE_LIMIT) * r_scr[...]
    pulled = pulled * (1.0 / (1.0 + jnp.exp(-raw)))
    pulled = jnp.concatenate([pulled, jnp.zeros((PAD - heads, rows), jnp.float32)], axis=0)
    d_scr[lanes : lanes + PAD, :] = pulled.astype(jnp.bfloat16)
    g_scr[...] += dot(d_scr[...], scaled)

    @pl.when(step == pl.num_programs(0) - 1)
    def _():
        grads = g_scr[...]
        div = div_ref[...].astype(jnp.float32)
        part = part_ref[...].astype(jnp.float32)
        div_slope = dot(energy_ref[...], grads, NN, HIGHEST)
        part_slope = dot(num_ref[...].astype(jnp.float32), m_ref[...], NN, HIGHEST)
        mixed = jnp.sum(div * div_slope + part * part_slope, axis=0, keepdims=True)
        mixed = mixed / scale_ref[...]
        full = dot(div, grads, NT, HIGHEST)
        width = full.shape[0] // heads
        energy = fold_heads(full[:, :lanes], heads, width, slices)
        tail = full[:, lanes : lanes + PAD]
        sharp = jnp.where(same_head(tail.shape, width, 1), tail, 0.0)
        sharp = jnp.sum(sharp, axis=1, keepdims=True)
        unit = 2 * width + 16
        for h in range(heads):
            base = (h // local) * block + (h % local) * unit
            own = slice(h * width, (h + 1) * width)
            out_ref[base : base + width, :] = div_slope[own].astype(jnp.bfloat16)
            out_ref[base + width : base + 2 * width, :] = part_slope[own].astype(
                jnp.bfloat16
            )
            pair = jnp.concatenate(
                [
                    energy[:, h * slices : (h + 1) * slices],
                    jnp.broadcast_to(sharp[own], (width, 128 - slices)),
                ],
                axis=1,
            )
            out_ref[base + 2 * width : base + unit, :] = jnp.concatenate(
                [pair[:16], pair[16:]], axis=1
            ).astype(jnp.bfloat16)
        for g in range(heads // local):
            base = g * block + local * unit
            rows_left = block - local * unit
            tail = gains_ref[...] + jnp.where(
                lax.broadcasted_iota(jnp.int32, gains_ref.shape, 0) == 0, mixed, 0.0
            )
            if rows_left > 8:
                tail = jnp.concatenate(
                    [tail, jnp.zeros((rows_left - 8, mixed.shape[1]), jnp.float32)], axis=0
                )
            out_ref[base : base + rows_left, :] = tail.astype(jnp.bfloat16)


def cost(units, rows, width):
    return pl.CostEstimate(
        flops=2 * units * rows * width * width,
        transcendentals=4 * rows * width,
        bytes_accessed=units * rows * width,
    )


def whole(shape):
    return pl.BlockSpec(shape, lambda i, *refs: (0,) * len(shape))


def params():
    return pltpu.CompilerParams(
        dimension_semantics=("arbitrary",), vmem_limit_bytes=56 * 1024 * 1024
    )


def token_attention(total_num, total_den, asking_projection, lookup_projection, content_projection):
    tokens = total_num / (total_den[:, :, None] + NORM_EPS)
    query_rows = jnp.einsum("hse,hef->hsf", tokens, asking_projection, precision=HIGHEST)
    key_rows = jnp.einsum("hse,hef->hsf", tokens, lookup_projection, precision=HIGHEST)
    value_rows = jnp.einsum("hse,hef->hsf", tokens, content_projection, precision=HIGHEST)
    scores = (
        jnp.einsum("hsf,htf->hst", query_rows, key_rows, precision=HIGHEST)
        * query_rows.shape[-1] ** (-0.5)
    )
    bounded_energies = SCORE_LIMIT * jnp.tanh(scores / SCORE_LIMIT)
    raised = jnp.exp(bounded_energies)
    attend = raised / jnp.sum(raised, axis=-1, keepdims=True)
    return jnp.einsum("hst,htf->hsf", attend, value_rows, precision=HIGHEST)


def block_diagonal(value):
    heads, rows, columns = value.shape
    eye = jnp.eye(heads, dtype=value.dtype)
    return (value[:, :, None, :] * eye[:, None, :, None]).reshape(heads * rows, heads * columns)


def body(
    mesh_signals,
    loss_sensitivity,
    divider_projection,
    partition_projection,
    sharpness_axis,
    partition_energies,
    asking_projection,
    lookup_projection,
    content_projection,
    prefocus_scale,
    emit_projection,
    premlp_scale,
    expand_factor,
    expand_offset,
    contract_factor,
):
    groups = lax.axis_size("head")
    member = lax.axis_index("head")
    rows = loss_sensitivity.shape[0]
    width = mesh_signals.shape[1]
    local, channels, slices = partition_energies.shape
    heads = local * groups
    lanes = heads * slices
    every_group = axis_groups("pts") + axis_groups("head")
    place = member.reshape(1).astype(jnp.int32)

    packed = pl.pallas_call(
        pack_kernel,
        out_shape=jax.ShapeDtypeStruct((groups, 3 * local * channels, width), jnp.float32),
        name="pack",
    )(
        divider_projection.T,
        partition_projection.T,
        sharpness_axis[None, :],
        partition_energies,
        asking_projection,
        lookup_projection,
        content_projection,
    )
    packed = lax.all_to_all(packed, "head", 0, 0, tiled=True)
    packed = packed.reshape(3 * heads * channels, width)
    square = jax.ShapeDtypeStruct((heads, channels, channels), jnp.float32)
    high, low, energy_rows, div_t, part_t, asking, lookup, content = pl.pallas_call(
        unpack_kernel,
        out_shape=[
            jax.ShapeDtypeStruct((lanes + PAD, width), jnp.bfloat16),
            jax.ShapeDtypeStruct((lanes + PAD, width), jnp.bfloat16),
            jax.ShapeDtypeStruct((heads * channels, lanes + PAD), jnp.float32),
            jax.ShapeDtypeStruct((heads * channels, width), jnp.bfloat16),
            jax.ShapeDtypeStruct((heads * channels, width), jnp.bfloat16),
            square,
            square,
            square,
        ],
        name="unpack",
    )(packed)

    tile = 1024
    steps = rows // tile
    total_rows = lanes + PAD
    row_block = pl.BlockSpec((tile, width), lambda i, *refs: (i, 0))
    own_block = pl.BlockSpec((tile, width), lambda i, place: (place[0] * steps + i, 0))
    column_block = pl.BlockSpec((lanes, tile), lambda i, *refs: (0, i))
    scaled = pl.pallas_call(
        norm_kernel,
        grid_spec=pltpu.PrefetchScalarGridSpec(
            num_scalar_prefetch=1,
            grid=(steps,),
            in_specs=[own_block, whole((1, width))],
            out_specs=row_block,
        ),
        out_shape=jax.ShapeDtypeStruct((rows, width), jnp.bfloat16),
        compiler_params=params(),
        cost_estimate=cost(8, rows, width),
        name="norm",
    )(place, mesh_signals, prefocus_scale[None, :])
    weights, moment, totals = pl.pallas_call(
        functools.partial(front_kernel, heads=heads, slices=slices, chunk=256),
        grid=(steps,),
        in_specs=[
            row_block,
            whole((total_rows, width)),
            whole((total_rows, width)),
            whole((heads * channels, width)),
        ],
        out_specs=[
            column_block,
            whole((lanes, width)),
            whole((channels + 8, lanes)),
        ],
        scratch_shapes=[
            pltpu.VMEM((total_rows, tile), jnp.float32),
            pltpu.VMEM((heads, tile), jnp.float32),
            pltpu.VMEM((lanes, 128), jnp.float32),
        ],
        out_shape=[
            jax.ShapeDtypeStruct((lanes, rows), jnp.bfloat16),
            jax.ShapeDtypeStruct((lanes, width), jnp.float32),
            jax.ShapeDtypeStruct((channels + 8, lanes), jnp.float32),
        ],
        compiler_params=params(),
        cost_estimate=cost(16, rows, width),
        name="front",
    )(scaled, high, low, part_t)

    totals = all_sum(totals, every_group)
    total_num = totals[:channels].reshape(channels, heads, slices).transpose(1, 2, 0)
    total_den = totals[channels].reshape(heads, slices)
    token_out, token_back = jax.vjp(
        token_attention, total_num, total_den, asking, lookup, content
    )
    token_low = token_out.astype(jnp.bfloat16)
    token_rows = block_diagonal(token_low.transpose(0, 2, 1))
    token_emit = lax.dot_general(
        token_rows, emit_projection, TN, preferred_element_type=jnp.float32
    ).astype(jnp.bfloat16)

    block_result, back_low, grads, gains, token_grad = pl.pallas_call(
        functools.partial(mixer_kernel, heads=heads, slices=slices),
        grid_spec=pltpu.PrefetchScalarGridSpec(
            num_scalar_prefetch=1,
            grid=(steps,),
            in_specs=[
                own_block,
                column_block,
                row_block,
                whole((lanes, width)),
                whole((1, width)),
                whole(expand_factor.shape),
                whole(expand_factor.shape[::-1]),
                whole((1, expand_offset.shape[0])),
                whole(contract_factor.shape),
                whole(contract_factor.shape[::-1]),
                whole(token_rows.shape),
                whole(emit_projection.shape),
            ],
            out_specs=[
                row_block,
                row_block,
                whole((3 * width, width)),
                whole((8, width)),
                whole((channels, lanes)),
            ],
            scratch_shapes=[
                pltpu.VMEM((2 * width, width), jnp.float32),
                pltpu.VMEM((lanes, width), jnp.float32),
                pltpu.VMEM((16, width), jnp.float32),
            ],
        ),
        out_shape=[
            jax.ShapeDtypeStruct((rows, width), jnp.bfloat16),
            jax.ShapeDtypeStruct((rows, width), jnp.bfloat16),
            jax.ShapeDtypeStruct((3 * width, width), jnp.bfloat16),
            jax.ShapeDtypeStruct((8, width), jnp.float32),
            jax.ShapeDtypeStruct((channels, lanes), jnp.float32),
        ],
        compiler_params=params(),
        cost_estimate=cost(26, rows, width),
        name="mixer",
    )(
        place,
        mesh_signals,
        weights,
        loss_sensitivity,
        token_emit,
        premlp_scale[None, :],
        expand_factor,
        expand_factor.T,
        expand_offset[None, :],
        contract_factor,
        contract_factor.T,
        token_rows,
        emit_projection,
    )

    for group in every_group:
        token_grad = group_sum(token_grad, group)
    token_grad = token_grad.reshape(channels, heads, slices).transpose(1, 2, 0)
    back_num, back_den, asking_slope, lookup_slope, content_slope = token_back(token_grad)
    num_low = block_diagonal(back_num.astype(jnp.bfloat16).transpose(0, 2, 1))
    feat_back = lax.dot_general(
        num_low, part_t, TN, preferred_element_type=jnp.float32
    ).astype(jnp.bfloat16)
    den_rows = jnp.broadcast_to(back_den.reshape(lanes, 1), (lanes, 128))

    everyone = ("head", "pts")
    grads = exchange_sum(grads, everyone)
    grads = gather(grads, everyone)

    unit = 2 * channels + 16
    grain = 8 * lax.axis_size("pts")
    block = -(-(local * unit + 8) // grain) * grain
    back_call = pl.pallas_call(
        functools.partial(back_kernel, heads=heads, slices=slices, chunk=256, local=local, block=block),
        grid=(steps,),
        in_specs=[
            row_block,
            row_block,
            whole((total_rows, width)),
            whole((total_rows, width)),
            whole((lanes, width)),
            whole((lanes, width)),
            whole((lanes, 128)),
            whole((lanes, width)),
            whole((heads * channels, total_rows)),
            whole((heads * channels, lanes)),
            whole((heads * channels, width)),
            whole((heads * channels, width)),
            whole((1, width)),
            whole((8, width)),
        ],
        out_specs=whole((groups * block, width)),
        scratch_shapes=[
            pltpu.VMEM((total_rows, tile), jnp.float32),
            pltpu.VMEM((lanes, tile), jnp.float32),
            pltpu.VMEM((heads, tile), jnp.float32),
            pltpu.VMEM((total_rows, tile), jnp.bfloat16),
            pltpu.VMEM((total_rows, width), jnp.float32),
        ],
        out_shape=jax.ShapeDtypeStruct((groups * block, width), jnp.bfloat16),
        compiler_params=params(),
        cost_estimate=cost(26, rows, width),
        name="back",
    )
    head_grads = back_call(
        scaled,
        back_low,
        high,
        low,
        token_emit,
        feat_back,
        den_rows,
        moment,
        energy_rows,
        num_low,
        div_t,
        part_t,
        prefocus_scale[None, :],
        gains,
    )

    head_grads, grads = lax.optimization_barrier((head_grads, grads))
    head_grads = gather(exchange_sum(head_grads, everyone), ("pts",))
    row = jax.ShapeDtypeStruct((1, width), jnp.float32)
    flat = jax.ShapeDtypeStruct((local * channels, width), jnp.float32)
    divider_slope, partition_slope, energy_slope, sharp_slope, scale_slope, premlp_slope, offset_slope = (
        pl.pallas_call(
            finish_kernel,
            out_shape=[
                flat,
                flat,
                jax.ShapeDtypeStruct((local, channels, slices), jnp.float32),
                jax.ShapeDtypeStruct((1, local * channels), jnp.float32),
                row,
                row,
                row,
            ],
            name="finish",
        )(head_grads)
    )

    def own_heads(value):
        return lax.dynamic_slice_in_dim(value, member * local, local, 0)

    return (
        block_result,
        divider_slope.T,
        partition_slope.T,
        sharp_slope.reshape(-1),
        energy_slope,
        own_heads(asking_slope),
        own_heads(lookup_slope),
        own_heads(content_slope),
        scale_slope.reshape(-1),
        grads[:width],
        premlp_slope.reshape(-1),
        grads[width : 2 * width],
        offset_slope.reshape(-1),
        grads[2 * width : 3 * width],
    )


def solution(mesh):
    in_specs = (
        P("pts", None),
        P(("pts", "head"), None),
        P(None, "head"),
        P(None, "head"),
        P("head"),
        P("head", None, None),
        P("head", None, None),
        P("head", None, None),
        P("head", None, None),
        P(),
        P(),
        P(),
        P(),
        P(),
        P(),
    )
    out_specs = (
        P(("pts", "head"), None),
        P(None, "head"),
        P(None, "head"),
        P("head"),
        P("head", None, None),
        P("head", None, None),
        P("head", None, None),
        P("head", None, None),
        P(),
        P(),
        P(),
        P(),
        P(),
        P(),
    )
    return jax.shard_map(body, mesh=mesh, in_specs=in_specs, out_specs=out_specs, check_vma=False)
```

profile of v0, /device:TPU:0, one launch (start us, length us, event | category | flops | bytes accessed | tf_op | source)
XLA Modules:
  0.0 188.9 jit_solution(1888431589627926615)
XLA Ops:
  0.6 1.9 %pack.1 = f32[4,192,256]{2,1,0:T(8,128)} custom-call(bf16[64,256]{1,0:T(8,128)(2,1)} %bitcast.75, bf16[64,256]{1,0:T(8,128)(2,1)} %bitcast.76, f32[1,64]{1,0:T(1,128)} %bitcast.77, f32[2,32,64]{2,1,0:T(8,128)} %energy_ref.1, f32[2,32,32]{2,1,0:T(8,128)} %ask_ref.1, f32[2,32,32]{2,1,0:T(8,128)} %look_ref.1, f32[2,32,32]{2,1,0:T(8,128)} %content_ref.1), custom_call_target="tpu_custom_call" | custom-call | tf_op jit(solution)/shard_map/pack/pallas_call | solution.py:495
  2.5 5.2 %all-to-all-start = ((f32[4,192,256]{2,1,0:T(8,128)}), f32[4,192,256]{2,1,0:T(8,128)S(1)}, u32[]{:S(2)}, u32[]{:S(2)}) async-start(f32[4,192,256]{2,1,0:T(8,128)} %pack.1), calls=%async_computation | async-start | bytes 1572864 | tf_op jit(solution)/shard_map/all_to_all | solution.py:508
  7.7 8.0 %norm.1.s_ref = bf16[8192,256]{1,0:T(8,128)(2,1)} custom-call(s32[1]{0:T(128)} %bitcast.member_ref, bf16[32768,256]{1,0:T(8,128)(2,1)} %x_ref.3, f32[1,256]{1,0:T(1,128)} %bitcast.82), custom_call_target="tpu_custom_call" | custom-call | flops 8589934592 | bytes 16777216 | tf_op jit(solution)/shard_map/norm/pallas_call | solution.py:532
  15.7 2.9 %all-to-all-done = f32[4,192,256]{2,1,0:T(8,128)S(1)} async-done(((f32[4,192,256]{2,1,0:T(8,128)}), f32[4,192,256]{2,1,0:T(8,128)S(1)}, u32[]{:S(2)}, u32[]{:S(2)}) %all-to-all-start) | async-done | bytes 786464 | tf_op jit(solution)/shard_map/all_to_all | solution.py:508
  18.6 0.9 copy-done
  19.4 2.9 %unpack.1 = (bf16[528,256]{1,0:T(8,128)(2,1)}, bf16[528,256]{1,0:T(8,128)(2,1)}, f32[256,528]{1,0:T(8,128)}, bf16[256,256]{1,0:T(8,128)(2,1)}, bf16[256,256]{1,0...) custom-call(f32[768,256]{1,0:T(8,128)} %bitcast.69), custom_call_target="tpu_custom_call" | custom-call | tf_op jit(solution)/shard_map/unpack/pallas_call | solution.py:511
  22.4 16.2 %front.1 = (bf16[512,8192]{1,0:T(8,128)(2,1)}, f32[512,256]{1,0:T(8,128)}, f32[40,512]{1,0:T(8,128)}) custom-call(bf16[8192,256]{1,0:T(8,128)(2,1)} %norm.1.s_ref, bf16[528,256]{1,0:T(8,128)(2,1)} %get-tuple-element.39.high_ref, bf16[528,256]{1,0:T(8,128)(2,1)} %get-tuple-element.40.low_ref, bf16[256,256]{1,0:T(8,128)(2,1)} %get-tuple-element.41.feat_ref.part_ref), custom_call_target="tpu_custom_call" | custom-call | flops 17179869184 | bytes 33554432 | tf_op jit(solution)/shard_map/front/pallas_call | solution.py:545
  38.6 1.5 collective-permute-done
  40.1 0.9 add.67
  41.0 1.7 collective-permute-start.1
  42.7 2.6 %collective-permute-start.2 = (f32[40,512]{1,0:T(8,128)S(1)}, f32[40,512]{1,0:T(8,128)S(1)}, u32[]{:S(2)}, u32[]{:S(2)}) collective-permute-start(f32[40,512]{1,0:T(8,128)S(1)} %add.67), channel_id=1, source_target_pairs={{0,16},{4,20},{8,24},{12,28},{16,0},{20,4},{24,8},{28,12},{1,17},{... | collective-permute-start | bytes 245768 | tf_op jit(solution)/shard_map/ppermute | solution.py:43
  45.4 0.8 copy.35
  46.2 0.8 copy.34
  47.0 5.2 %collective-permute-done.2 = f32[40,512]{1,0:T(8,128)S(1)} collective-permute-done((f32[40,512]{1,0:T(8,128)S(1)}, f32[40,512]{1,0:T(8,128)S(1)}, u32[]{:S(2)}, u32[]{:S(2)}) %collective-permute-start.2) | collective-permute-done | bytes 81952 | tf_op jit(solution)/shard_map/ppermute | solution.py:43
  52.2 1.5 collective-permute-start.4
  53.6 0.6 collective-permute-start.5
  54.2 1.5 collective-permute-start.6
  55.7 1.2 collective-permute-done.4
  56.9 1.1 collective-permute-done.5
  58.1 1.5 collective-permute-done.6
  59.8 0.4 fusion.20
  60.2 0.4 fusion.21
  60.6 0.4 fusion.22
  61.0 0.6 fusion.2
  61.6 0.4 convolution_convert_fusion.2
  62.1 0.3 mul.100.token_ref
  62.5 1.0 convolution_convert_fusion.1.te_ref
  63.4 27.0 %mixer.1 = (bf16[8192,256]{1,0:T(8,128)(2,1)}, bf16[8192,256]{1,0:T(8,128)(2,1)}, bf16[768,256]{1,0:T(8,128)(2,1)}, f32[8,256]{1,0:T(8,128)}, f32[32,512]{1,0:T(8,128)}) custom-call(s32[1]{0:T(128)} %bitcast.member_ref, bf16[32768,256]{1,0:T(8,128)(2,1)} %x_ref.3, bf16[512,8192]{1,0:T(8,128)(2,1)} %get-tuple-element.42.w_ref, bf16[8192,256]{1,0:T(8,128)(2,1)} %loss_ref.1, ...), custom_call_target="tpu_custom_call" | custom-call | flops 27917287424 | bytes 54525952 | tf_op jit(solution)/shard_map/mixer/pallas_call | solution.py:586
  90.5 1.5 collective-permute-done.7
  92.0 0.8 add.77
  92.8 2.6 %collective-permute-start.10 = (f32[32,512]{1,0:T(8,128)S(1)}, f32[32,512]{1,0:T(8,128)S(1)}, u32[]{:S(2)}, u32[]{:S(2)}) collective-permute-start(f32[32,512]{1,0:T(8,128)S(1)} %add.77), channel_id=1, source_target_pairs={{0,24},{4,28},{8,16},{12,20},{16,8},{20,12},{24,0},{28,4},{1,25},{... | collective-permute-start | bytes 196616 | tf_op jit(solution)/shard_map/ppermute | solution.py:43
  95.4 0.5 collective-permute-start.8
  95.9 1.3 collective-permute-start.9
  97.3 2.3 %collective-permute-done.10 = f32[32,512]{1,0:T(8,128)S(1)} collective-permute-done((f32[32,512]{1,0:T(8,128)S(1)}, f32[32,512]{1,0:T(8,128)S(1)}, u32[]{:S(2)}, u32[]{:S(2)}) %collective-permute-start.10) | collective-permute-done | bytes 65568 | tf_op jit(solution)/shard_map/ppermute | solution.py:43
  99.5 1.9 %collective-permute-done.8 = f32[32,512]{1,0:T(8,128)S(1)} collective-permute-done((f32[32,512]{1,0:T(8,128)S(1)}, f32[32,512]{1,0:T(8,128)S(1)}, u32[]{:S(2)}, u32[]{:S(2)}) %collective-permute-start.8) | collective-permute-done | bytes 65568 | tf_op jit(solution)/shard_map/ppermute | solution.py:43
  101.5 0.9 collective-permute-done.9
  102.4 1.6 collective-permute-start.11
  103.9 0.6 collective-permute-start.12
  104.5 1.4 collective-permute-start.13
  105.9 3.9 %all-to-all-start.1 = ((bf16[32,24,256]{2,1,0:T(8,128)(2,1)}), bf16[32,24,256]{2,1,0:T(8,128)(2,1)S(1)}, u32[]{:S(2)}, u32[]{:S(2)}) async-start(bf16[32,24,256]{2,1,0:T(8,128)(2,1)} %bitcast.71), calls=%async_computation.1 | async-start | bytes 786432 | tf_op jit(solution)/shard_map/all_to_all | solution.py:68
  110.0 0.5 fusion.5
  110.5 0.6 multiply_reduce_fusion
  111.3 0.5 fusion.25
  111.8 0.4 fusion.26
  113.1 0.3 mul.112.num_ref
  113.6 1.0 convolution_convert_fusion.fb_ref
  114.5 8.6 %all-to-all-done.1 = bf16[32,24,256]{2,1,0:T(8,128)(2,1)S(1)} async-done(((bf16[32,24,256]{2,1,0:T(8,128)(2,1)}), bf16[32,24,256]{2,1,0:T(8,128)(2,1)S(1)}, u32[]{:S(2)}, u32[]{:S(2)}) %all-to-all-start.1) | async-done | bytes 393248 | tf_op jit(solution)/shard_map/all_to_all | solution.py:68
  123.2 0.9 broadcast_in_dim.44
  124.1 2.6 %all-to-all-start.2 = ((f32[32,24,256]{2,1,0:T(8,128)}), f32[32,24,256]{2,1,0:T(8,128)S(1)}, u32[]{:S(2)}, u32[]{:S(2)}) async-start(f32[32,24,256]{2,1,0:T(8,128)} %broadcast_in_dim.44), calls=%async_computation.2 | async-start | bytes 1572864 | tf_op jit(solution)/shard_map/all_to_all | solution.py:76
  126.7 0.8 broadcast_in_dim.21.den_ref
  127.6 27.3 %back.1 = bf16[768,256]{1,0:T(8,128)(2,1)} custom-call(bf16[8192,256]{1,0:T(8,128)(2,1)} %norm.1.s_ref, bf16[8192,256]{1,0:T(8,128)(2,1)} %get-tuple-element.48.back_ref, bf16[528,256]{1,0:T(8,128)(2,1)} %get-tuple-element.39.high_ref, bf16[528,256]{1,0:T(8,128)(2,1)} %get-tuple-element.40.low_ref, bf16[512,256]{1,0:T(8,128)(2,1)} %convolution_convert_fusion.1.te_ref, ...), custom_call_target="tpu_custom_call" | custom-call | flops 27917287424 | bytes 54525952 | tf_op jit(solution)/shard_map/back/pallas_call | solution.py:693
  154.9 5.8 %all-to-all-start.3 = ((bf16[32,24,256]{2,1,0:T(8,128)(2,1)}), bf16[32,24,256]{2,1,0:T(8,128)(2,1)S(1)}, u32[]{:S(2)}, u32[]{:S(2)}) async-start(bf16[32,24,256]{2,1,0:T(8,128)(2,1)} %bitcast.72), calls=%async_computation.3 | async-start | bytes 786432 | tf_op jit(solution)/shard_map/all_to_all | solution.py:68
  160.8 0.3 fusion.18
  161.1 0.3 fusion.17
  161.5 0.6 constant_dynamic-slice_fusion
  162.1 0.3 fusion.19
  162.5 11.7 %all-to-all-done.3 = bf16[32,24,256]{2,1,0:T(8,128)(2,1)S(1)} async-done(((bf16[32,24,256]{2,1,0:T(8,128)(2,1)}), bf16[32,24,256]{2,1,0:T(8,128)(2,1)S(1)}, u32[]{:S(2)}, u32[]{:S(2)}) %all-to-all-start.3) | async-done | bytes 393248 | tf_op jit(solution)/shard_map/all_to_all | solution.py:68
  174.3 0.7 broadcast_in_dim.45
  175.0 3.4 %all-to-all-start.4 = ((f32[8,24,256]{2,1,0:T(8,128)}), f32[8,24,256]{2,1,0:T(8,128)S(1)}, u32[]{:S(2)}, u32[]{:S(2)}) async-start(f32[8,24,256]{2,1,0:T(8,128)} %broadcast_in_dim.45), calls=%async_computation.4 | async-start | bytes 393216 | tf_op jit(solution)/shard_map/all_to_all | solution.py:76
  178.4 0.6 constant_dynamic-slice_fusion.2
  179.0 0.9 fusion.23
  179.9 6.7 %all-to-all-done.4 = f32[8,24,256]{2,1,0:T(8,128)S(1)} async-done(((f32[8,24,256]{2,1,0:T(8,128)}), f32[8,24,256]{2,1,0:T(8,128)S(1)}, u32[]{:S(2)}, u32[]{:S(2)}) %all-to-all-start.4) | async-done | bytes 196640 | tf_op jit(solution)/shard_map/all_to_all | solution.py:76
  186.6 0.7 copy-done.3
  187.3 1.6 finish.1
  (52 shorter events, 2.1 us)
Async XLA Ops:
  2.5 16.0 %all-to-all-start = ((f32[4,192,256]{2,1,0:T(8,128)}), f32[4,192,256]{2,1,0:T(8,128)S(1)}, u32[]{:S(2)}, u32[]{:S(2)}) async-start(f32[4,192,256]{2,1,0:T(8,128)} %pack.1), calls=%async_computation | async-start | bytes 1572864 | tf_op jit(solution)/shard_map/all_to_all | solution.py:508
  18.6 0.9 copy-start
  22.3 23.1 %copy-start.8 = (bf16[256,256]{1,0:T(8,128)(2,1)S(1)}, bf16[256,256]{1,0:T(8,128)(2,1)}, u32[]{:S(2)}) copy-start(bf16[256,256]{1,0:T(8,128)(2,1)} %contract_ref.1) | copy-start | bytes 393220
  22.3 23.9 %copy-start.7 = (bf16[256,256]{1,0:T(8,128)(2,1)S(1)}, bf16[256,256]{1,0:T(8,128)(2,1)}, u32[]{:S(2)}) copy-start(bf16[256,256]{1,0:T(8,128)(2,1)} %expand_ref.1) | copy-start | bytes 393220
  22.3 37.4 %copy-start.9 = (f32[8,32,32]{2,1,0:T(8,128)S(1)}, f32[8,32,32]{2,1,0:T(8,128)}, u32[]{:S(2)}) copy-start(f32[8,32,32]{2,1,0:T(8,128)} %get-tuple-element.46) | copy-start | bytes 98308
  22.4 37.8 %copy-start.10 = (f32[8,32,32]{2,1,0:T(8,128)S(1)}, f32[8,32,32]{2,1,0:T(8,128)}, u32[]{:S(2)}) copy-start(f32[8,32,32]{2,1,0:T(8,128)} %get-tuple-element.45) | copy-start | bytes 98308
  22.4 38.2 %copy-start.6 = (f32[8,32,32]{2,1,0:T(8,128)S(1)}, f32[8,32,32]{2,1,0:T(8,128)}, u32[]{:S(2)}) copy-start(f32[8,32,32]{2,1,0:T(8,128)} %get-tuple-element.44) | copy-start | bytes 98308
  38.5 23.9 %copy-start.4 = (bf16[256,256]{1,0:T(8,128)(2,1)S(1)}, bf16[256,256]{1,0:T(8,128)(2,1)}, u32[]{:S(2)}) copy-start(bf16[256,256]{1,0:T(8,128)(2,1)} %emit_ref.1) | copy-start | bytes 393220
  38.5 1.6 collective-permute-start
  41.0 6.0 %collective-permute-start.1 = (f32[40,512]{1,0:T(8,128)S(1)}, f32[40,512]{1,0:T(8,128)S(1)}, u32[]{:S(2)}, u32[]{:S(2)}) collective-permute-start(f32[40,512]{1,0:T(8,128)S(1)} %add.67), channel_id=1, source_target_pairs={{0,8},{4,12},{8,0},{12,4},{16,24},{20,28},{24,16},{28,20},{1,9},{5... | collective-permute-start | bytes 245768 | tf_op jit(solution)/shard_map/ppermute | solution.py:43
  42.7 9.5 %collective-permute-start.2 = (f32[40,512]{1,0:T(8,128)S(1)}, f32[40,512]{1,0:T(8,128)S(1)}, u32[]{:S(2)}, u32[]{:S(2)}) collective-permute-start(f32[40,512]{1,0:T(8,128)S(1)} %add.67), channel_id=1, source_target_pairs={{0,16},{4,20},{8,24},{12,28},{16,0},{20,4},{24,8},{28,12},{1,17},{... | collective-permute-start | bytes 245768 | tf_op jit(solution)/shard_map/ppermute | solution.py:43
  45.3 6.9 %collective-permute-start.3 = (f32[40,512]{1,0:T(8,128)S(1)}, f32[40,512]{1,0:T(8,128)S(1)}, u32[]{:S(2)}, u32[]{:S(2)}) collective-permute-start(f32[40,512]{1,0:T(8,128)S(1)} %add.67), channel_id=1, source_target_pairs={{0,24},{4,28},{8,16},{12,20},{16,8},{20,12},{24,0},{28,4},{1,25},{... | collective-permute-start | bytes 245768 | tf_op jit(solution)/shard_map/ppermute | solution.py:43
  52.2 4.8 %collective-permute-start.4 = (f32[40,512]{1,0:T(8,128)S(1)}, f32[40,512]{1,0:T(8,128)S(1)}, u32[]{:S(2)}, u32[]{:S(2)}) collective-permute-start(f32[40,512]{1,0:T(8,128)S(1)} %add_add_fusion.1), channel_id=1, source_target_pairs={{0,1},{1,0},{2,3},{3,2},{4,5},{5,4},{6,7},{7,6},{8,9},{9,8},{10,11... | collective-permute-start | bytes 245768 | tf_op jit(solution)/shard_map/ppermute | solution.py:43
  53.6 4.4 %collective-permute-start.5 = (f32[40,512]{1,0:T(8,128)S(1)}, f32[40,512]{1,0:T(8,128)S(1)}, u32[]{:S(2)}, u32[]{:S(2)}) collective-permute-start(f32[40,512]{1,0:T(8,128)S(1)} %add_add_fusion.1), channel_id=1, source_target_pairs={{0,2},{1,3},{2,0},{3,1},{4,6},{5,7},{6,4},{7,5},{8,10},{9,11},{10,... | collective-permute-start | bytes 245768 | tf_op jit(solution)/shard_map/ppermute | solution.py:43
  54.2 5.3 %collective-permute-start.6 = (f32[40,512]{1,0:T(8,128)S(1)}, f32[40,512]{1,0:T(8,128)S(1)}, u32[]{:S(2)}, u32[]{:S(2)}) collective-permute-start(f32[40,512]{1,0:T(8,128)S(1)} %add_add_fusion.1), channel_id=1, source_target_pairs={{0,3},{1,2},{2,1},{3,0},{4,7},{5,6},{6,5},{7,4},{8,11},{9,10},{10,... | collective-permute-start | bytes 245768 | tf_op jit(solution)/shard_map/ppermute | solution.py:43
  62.5 1.0 copy-start.2
  90.4 1.5 collective-permute-start.7
  92.8 20.7 %copy-start.5 = (bf16[256,256]{1,0:T(8,128)(2,1)S(1)}, bf16[256,256]{1,0:T(8,128)(2,1)}, u32[]{:S(2)}) copy-start(bf16[256,256]{1,0:T(8,128)(2,1)} %get-tuple-element.41.feat_ref.part_ref) | copy-start | bytes 393220
  92.8 6.7 %collective-permute-start.10 = (f32[32,512]{1,0:T(8,128)S(1)}, f32[32,512]{1,0:T(8,128)S(1)}, u32[]{:S(2)}, u32[]{:S(2)}) collective-permute-start(f32[32,512]{1,0:T(8,128)S(1)} %add.77), channel_id=1, source_target_pairs={{0,24},{4,28},{8,16},{12,20},{16,8},{20,12},{24,0},{28,4},{1,25},{... | collective-permute-start | bytes 196616 | tf_op jit(solution)/shard_map/ppermute | solution.py:43
  95.4 6.0 %collective-permute-start.8 = (f32[32,512]{1,0:T(8,128)S(1)}, f32[32,512]{1,0:T(8,128)S(1)}, u32[]{:S(2)}, u32[]{:S(2)}) collective-permute-start(f32[32,512]{1,0:T(8,128)S(1)} %add.77), channel_id=1, source_target_pairs={{0,8},{4,12},{8,0},{12,4},{16,24},{20,28},{24,16},{28,20},{1,9},{5... | collective-permute-start | bytes 196616 | tf_op jit(solution)/shard_map/ppermute | solution.py:43
  95.9 6.4 %collective-permute-start.9 = (f32[32,512]{1,0:T(8,128)S(1)}, f32[32,512]{1,0:T(8,128)S(1)}, u32[]{:S(2)}, u32[]{:S(2)}) collective-permute-start(f32[32,512]{1,0:T(8,128)S(1)} %add.77), channel_id=1, source_target_pairs={{0,16},{4,20},{8,24},{12,28},{16,0},{20,4},{24,8},{28,12},{1,17},{... | collective-permute-start | bytes 196616 | tf_op jit(solution)/shard_map/ppermute | solution.py:43
  102.4 7.5 %collective-permute-start.11 = (f32[32,512]{1,0:T(8,128)S(1)}, f32[32,512]{1,0:T(8,128)S(1)}, u32[]{:S(2)}, u32[]{:S(2)}) collective-permute-start(f32[32,512]{1,0:T(8,128)S(1)} %add_add_fusion.3), channel_id=1, source_target_pairs={{0,1},{1,0},{2,3},{3,2},{4,5},{5,4},{6,7},{7,6},{8,9},{9,8},{10,11... | collective-permute-start | bytes 196616 | tf_op jit(solution)/shard_map/ppermute | solution.py:43
  103.9 5.9 %collective-permute-start.12 = (f32[32,512]{1,0:T(8,128)S(1)}, f32[32,512]{1,0:T(8,128)S(1)}, u32[]{:S(2)}, u32[]{:S(2)}) collective-permute-start(f32[32,512]{1,0:T(8,128)S(1)} %add_add_fusion.3), channel_id=1, source_target_pairs={{0,2},{1,3},{2,0},{3,1},{4,6},{5,7},{6,4},{7,5},{8,10},{9,11},{10,... | collective-permute-start | bytes 196616 | tf_op jit(solution)/shard_map/ppermute | solution.py:43
  104.5 5.4 %collective-permute-start.13 = (f32[32,512]{1,0:T(8,128)S(1)}, f32[32,512]{1,0:T(8,128)S(1)}, u32[]{:S(2)}, u32[]{:S(2)}) collective-permute-start(f32[32,512]{1,0:T(8,128)S(1)} %add_add_fusion.3), channel_id=1, source_target_pairs={{0,3},{1,2},{2,1},{3,0},{4,7},{5,6},{6,5},{7,4},{8,11},{9,10},{10,... | collective-permute-start | bytes 196616 | tf_op jit(solution)/shard_map/ppermute | solution.py:43
  105.9 17.2 %all-to-all-start.1 = ((bf16[32,24,256]{2,1,0:T(8,128)(2,1)}), bf16[32,24,256]{2,1,0:T(8,128)(2,1)S(1)}, u32[]{:S(2)}, u32[]{:S(2)}) async-start(bf16[32,24,256]{2,1,0:T(8,128)(2,1)} %bitcast.71), calls=%async_computation.1 | async-start | bytes 786432 | tf_op jit(solution)/shard_map/all_to_all | solution.py:68
  113.5 14.1 %copy-start.1 = (bf16[256,512]{1,0:T(8,128)(2,1)}, bf16[256,512]{1,0:T(8,128)(2,1)S(1)}, u32[]{:S(2)}) copy-start(bf16[256,512]{1,0:T(8,128)(2,1)S(1)} %mul.112.num_ref) | copy-start | bytes 786436
  124.1 30.8 %all-to-all-start.2 = ((f32[32,24,256]{2,1,0:T(8,128)}), f32[32,24,256]{2,1,0:T(8,128)S(1)}, u32[]{:S(2)}, u32[]{:S(2)}) async-start(f32[32,24,256]{2,1,0:T(8,128)} %broadcast_in_dim.44), calls=%async_computation.2 | async-start | bytes 1572864 | tf_op jit(solution)/shard_map/all_to_all | solution.py:76
  154.9 19.3 %all-to-all-start.3 = ((bf16[32,24,256]{2,1,0:T(8,128)(2,1)}), bf16[32,24,256]{2,1,0:T(8,128)(2,1)S(1)}, u32[]{:S(2)}, u32[]{:S(2)}) async-start(bf16[32,24,256]{2,1,0:T(8,128)(2,1)} %bitcast.72), calls=%async_computation.3 | async-start | bytes 786432 | tf_op jit(solution)/shard_map/all_to_all | solution.py:68
  175.0 11.6 %all-to-all-start.4 = ((f32[8,24,256]{2,1,0:T(8,128)}), f32[8,24,256]{2,1,0:T(8,128)S(1)}, u32[]{:S(2)}, u32[]{:S(2)}) async-start(f32[8,24,256]{2,1,0:T(8,128)} %broadcast_in_dim.45), calls=%async_computation.4 | async-start | bytes 393216 | tf_op jit(solution)/shard_map/all_to_all | solution.py:76
  186.6 0.7 copy-start.3
where the time goes:
time: 190 us; the launch traced here: 189 us
  Pallas kernels  84.9 us (45%)
  waiting for transfers between devices  46.9 us (25%)
  starting transfers between devices  37.1 us (20%)
  local copies, waits for them, and re-layouts  8.71 us (5%)
  matrix products  8.02 us (4%)
  other arithmetic  2.35 us (1%)
    pallas_call x1, Pallas kernels, body(): back_call(scaled, back_low, high, low, token_emit, feat_back, den_rows, m...  27.3 us
    pallas_call x1, Pallas kernels, body(): pl.pallas_call(functools.partial(mixer_kernel, heads=heads, slices=slices...  27 us
    all_to_all x2, waiting for transfers between devices, exchange_sum(): lax.all_to_all(value.reshape(count, block, value.shape[1]), axes, 0, 0, t...  20.3 us
    ppermute x14, waiting for transfers between devices, swap(): return lax.ppermute(value, axis, [(i, i ^ distance) for i in range(size)])  17 us
    ppermute x14, starting transfers between devices, swap(): return lax.ppermute(value, axis, [(i, i ^ distance) for i in range(size)])  16.2 us
    pallas_call x1, Pallas kernels, body(): pl.pallas_call(functools.partial(front_kernel, heads=heads, slices=slices...  16.2 us
    all_to_all x2, starting transfers between devices, exchange_sum(): lax.all_to_all(value.reshape(count, block, value.shape[1]), axes, 0, 0, t...  9.76 us
    pallas_call x1, Pallas kernels, body(): pl.pallas_call(norm_kernel, grid_spec=pltpu.PrefetchScalarGridSpec(num_sc...  7.96 us
  transfers between devices with their start and end apart: 19, of which 13 were waited for; matrix products, arithmetic and copies ran while one was open for 5% of the time, Pallas kernels for 19%

commit v1 on v0

--- a/solution.py
+++ b/solution.py
@@ -23,6 +23,15 @@
 
 def dot(a, b, numbers=NN, precision=None):
     return lax.dot_general(a, b, numbers, precision=precision, preferred_element_type=jnp.float32)
+
+
+def halves(value):
+    high = value.astype(jnp.bfloat16)
+    return high, (value - high.astype(jnp.float32)).astype(jnp.bfloat16)
+
+
+def dot_split(a, b, numbers=NN):
+    return dot(a, b[0], numbers) + dot(a, b[1], numbers)
 
 
 def axis_groups(axis):
@@ -127,10 +136,10 @@
 
 
 def unpack_kernel(
-    all_ref, high_ref, low_ref, energy_ref, div_ref, part_ref, ask_ref, look_ref, content_ref
+    all_ref, pair_ref, energy_ref, div_ref, part_ref, ask_ref, look_ref, content_ref
 ):
     heads, channels, _ = ask_ref.shape
-    lanes = high_ref.shape[0] - PAD
+    lanes = pair_ref.shape[0] - PAD
     slices = lanes // heads
     energy_ref[...] = jnp.zeros_like(energy_ref)
     for h in range(heads):
@@ -146,9 +155,7 @@
         spot = slices + 3 * channels
         energy_ref[own, lanes + h : lanes + h + 1] = rest[:, spot : spot + 1]
     logits_of = dot(energy_ref[...], div_ref[...].astype(jnp.float32), TN, HIGHEST)
-    high = logits_of.astype(jnp.bfloat16)
-    high_ref[...] = high
-    low_ref[...] = (logits_of - high.astype(jnp.float32)).astype(jnp.bfloat16)
+    pair_ref[...] = jnp.concatenate(halves(logits_of), axis=1)
 
 
 def finish_kernel(
@@ -186,8 +193,7 @@
 
 def front_kernel(
     s_ref,
-    high_ref,
-    low_ref,
+    pair_ref,
     feat_ref,
     w_ref,
     m_ref,
@@ -209,7 +215,7 @@
         den_scr[...] = jnp.zeros_like(den_scr)
 
     scaled = s_ref[...]
-    z_scr[...] = dot(high_ref[...], scaled, NT) + dot(low_ref[...], scaled, NT)
+    z_scr[...] = dot(pair_ref[...], jnp.concatenate([scaled, scaled], axis=1), NT)
     r_scr[...] = sharp_terms(z_scr[lanes : lanes + heads, :]) * (1.0 / SCORE_LIMIT)
     rows = s_ref.shape[0]
     for h in range(heads):
@@ -228,11 +234,11 @@
 
     @pl.when(step == pl.num_programs(0) - 1)
     def _():
-        full = dot(feat_ref[...].astype(jnp.float32), m_ref[...], NT, HIGHEST)
+        full = dot_split(feat_ref[...], halves(m_ref[...]), NT)
         width = full.shape[0] // heads
         tot_ref[0:width, :] = fold_heads(full, heads, width, slices)
-        ones = jnp.ones((8, 128), jnp.float32)
-        tot_ref[width : width + 8, :] = dot(ones, den_scr[...], NT, HIGHEST)
+        ones = jnp.ones((8, 128), jnp.bfloat16)
+        tot_ref[width : width + 8, :] = dot_split(ones, halves(den_scr[...]), NT)
 
 
 def mixer_kernel(
@@ -280,18 +286,15 @@
     gain = gain_ref[...]
     normed = (normal * gain).astype(jnp.bfloat16)
     inner = dot(normed, expand_ref[...]) + offset_ref[...]
-    square = inner * inner
-    bent = jnp.tanh(GELU_SCALE * inner * (1.0 + GELU_CUBE * square))
-    half = 0.5 * (1.0 + bent)
-    active = (inner * half).astype(jnp.bfloat16)
-    slope = half + 0.5 * inner * (1.0 - bent * bent) * (
-        GELU_SCALE + (3.0 * GELU_CUBE * GELU_SCALE) * square
-    )
+    cubic = (GELU_CUBE * GELU_SCALE) * (inner * inner)
+    half = 0.5 * jnp.tanh(inner * (GELU_SCALE + cubic)) + 0.5
+    gelu = inner * half
+    active = gelu.astype(jnp.bfloat16)
+    slope = half + (gelu - gelu * half) * (2.0 * GELU_SCALE + 6.0 * cubic)
     block_ref[...] = (residual + dot(active, contract_ref[...])).astype(jnp.bfloat16)
     back_inner = dot(loss, contract_t_ref[...]) * slope
     back_low = back_inner.astype(jnp.bfloat16)
     back_normed = dot(back_low, expand_t_ref[...])
-    gained = back_normed * normal
     pulled = back_normed * gain
     mean_pull = jnp.mean(pulled, axis=1, keepdims=True)
     mean_gain = jnp.mean(pulled * normal, axis=1, keepdims=True)
@@ -301,28 +304,27 @@
     acc_scr[0:width, :] += dot(normed, back_low, TN)
     acc_scr[width : 2 * width, :] += dot(active, loss, TN)
     rows = x_ref.shape[0]
-    gain_scr[0:8, :] += jnp.sum(gained.reshape(rows // 8, 8, width), axis=0)
-    gain_scr[8:16, :] += jnp.sum(back_inner.reshape(rows // 8, 8, width), axis=0)
+    gain_scr[...] += jnp.sum(back_inner.reshape(rows // 8, 8, width), axis=0)
     wr_scr[...] += dot(weights, back)
 
     @pl.when(step == pl.num_programs(0) - 1)
     def _():
-        grads_ref[0:width, :] = dot(
-            token_ref[...].astype(jnp.float32), wr_scr[...], NN, HIGHEST
-        ).astype(jnp.bfloat16)
+        pieces = halves(wr_scr[...])
+        grads_ref[0:width, :] = dot_split(token_ref[...], pieces).astype(jnp.bfloat16)
         grads_ref[width : 3 * width, :] = acc_scr[...].astype(jnp.bfloat16)
-        full = dot(emit_ref[...].astype(jnp.float32), wr_scr[...], NT, HIGHEST)
+        full = dot_split(emit_ref[...], pieces, NT)
         tg_ref[...] = fold_heads(full, heads, full.shape[0] // heads, slices)
         gains_ref[...] = jnp.zeros_like(gains_ref)
-        gains_ref[1:2, :] = jnp.sum(gain_scr[0:8, :], axis=0, keepdims=True)
-        gains_ref[2:3, :] = jnp.sum(gain_scr[8:16, :], axis=0, keepdims=True)
+        product = halves(expand_ref[...].astype(jnp.float32) * acc_scr[0:width, :])
+        total = dot_split(jnp.ones((8, product[0].shape[1]), jnp.bfloat16), product, NT)
+        gains_ref[1:2, :] = total[0:1] / gain
+        gains_ref[2:3, :] = jnp.sum(gain_scr[...], axis=0, keepdims=True)
 
 
 def back_kernel(
     s_ref,
     back_ref,
-    high_ref,
-    low_ref,
+    pair_ref,
     te_ref,
     fb_ref,
     den_ref,
@@ -355,8 +357,12 @@
         d_scr[...] = jnp.zeros_like(d_scr)
 
     scaled = s_ref[...]
-    z_scr[...] = dot(high_ref[...], scaled, NT) + dot(low_ref[...], scaled, NT)
-    b_scr[...] = dot(te_ref[...], back_ref[...], NT) + dot(fb_ref[...], scaled, NT)
+    z_scr[...] = dot(pair_ref[...], jnp.concatenate([scaled, scaled], axis=1), NT)
+    b_scr[...] = dot(
+        jnp.concatenate([te_ref[...], fb_ref[...]], axis=1),
+        jnp.concatenate([back_ref[...], scaled], axis=1),
+        NT,
+    )
     raw = z_scr[lanes : lanes + heads, :]
     r_scr[...] = sharp_terms(raw)
     rows = s_ref.shape[0]
@@ -385,11 +391,13 @@
         grads = g_scr[...]
         div = div_ref[...].astype(jnp.float32)
         part = part_ref[...].astype(jnp.float32)
-        div_slope = dot(energy_ref[...], grads, NN, HIGHEST)
-        part_slope = dot(num_ref[...].astype(jnp.float32), m_ref[...], NN, HIGHEST)
+        pieces = halves(grads)
+        energy_high, energy_low = halves(energy_ref[...])
+        div_slope = dot_split(energy_high, pieces) + dot(energy_low, pieces[0])
+        part_slope = dot_split(num_ref[...], halves(m_ref[...]))
         mixed = jnp.sum(div * div_slope + part * part_slope, axis=0, keepdims=True)
         mixed = mixed / scale_ref[...]
-        full = dot(div, grads, NT, HIGHEST)
+        full = dot_split(div_ref[...], pieces, NT)
         width = full.shape[0] // heads
         energy = fold_heads(full[:, :lanes], heads, width, slices)
         tail = full[:, lanes : lanes + PAD]
@@ -508,11 +516,10 @@
     packed = lax.all_to_all(packed, "head", 0, 0, tiled=True)
     packed = packed.reshape(3 * heads * channels, width)
     square = jax.ShapeDtypeStruct((heads, channels, channels), jnp.float32)
-    high, low, energy_rows, div_t, part_t, asking, lookup, content = pl.pallas_call(
+    pair, energy_rows, div_t, part_t, asking, lookup, content = pl.pallas_call(
         unpack_kernel,
         out_shape=[
-            jax.ShapeDtypeStruct((lanes + PAD, width), jnp.bfloat16),
-            jax.ShapeDtypeStruct((lanes + PAD, width), jnp.bfloat16),
+            jax.ShapeDtypeStruct((lanes + PAD, 2 * width), jnp.bfloat16),
             jax.ShapeDtypeStruct((heads * channels, lanes + PAD), jnp.float32),
             jax.ShapeDtypeStruct((heads * channels, width), jnp.bfloat16),
             jax.ShapeDtypeStruct((heads * channels, width), jnp.bfloat16),
@@ -523,7 +530,7 @@
         name="unpack",
     )(packed)
 
-    tile = 1024
+    tile = 2048
     steps = rows // tile
     total_rows = lanes + PAD
     row_block = pl.BlockSpec((tile, width), lambda i, *refs: (i, 0))
@@ -547,8 +554,7 @@
         grid=(steps,),
         in_specs=[
             row_block,
-            whole((total_rows, width)),
-            whole((total_rows, width)),
+            whole((total_rows, 2 * width)),
             whole((heads * channels, width)),
         ],
         out_specs=[
@@ -569,7 +575,7 @@
         compiler_params=params(),
         cost_estimate=cost(16, rows, width),
         name="front",
-    )(scaled, high, low, part_t)
+    )(scaled, pair, part_t)
 
     totals = all_sum(totals, every_group)
     total_num = totals[:channels].reshape(channels, heads, slices).transpose(1, 2, 0)
@@ -612,7 +618,7 @@
             scratch_shapes=[
                 pltpu.VMEM((2 * width, width), jnp.float32),
                 pltpu.VMEM((lanes, width), jnp.float32),
-                pltpu.VMEM((16, width), jnp.float32),
+                pltpu.VMEM((8, width), jnp.float32),
             ],
         ),
         out_shape=[
@@ -664,8 +670,7 @@
         in_specs=[
             row_block,
             row_block,
-            whole((total_rows, width)),
-            whole((total_rows, width)),
+            whole((total_rows, 2 * width)),
             whole((lanes, width)),
             whole((lanes, width)),
             whole((lanes, 128)),
@@ -693,8 +698,7 @@
     head_grads = back_call(
         scaled,
         back_low,
-        high,
-        low,
+        pair,
         token_emit,
         feat_back,
         den_rows,

time: 190 us -> 181 us (0.953)
  Pallas kernels: 84.9 us -> 74.5 us
    pallas_call x1, Pallas kernels: 27.3 us -> 22.6 us  [body(): back_call(scaled, back_low, pair, token_emit, feat_back, den_rows, moment...]
    pallas_call x1, Pallas kernels: 16.2 us -> 14 us  [body(): pl.pallas_call(functools.partial(front_kernel, heads=heads, slices=slices...]
  transfers between devices with their start and end apart: 19 -> 19, of which waited for: 13 -> 13; matrix products, arithmetic and copies ran while one was open for 5% -> 6% of each run, Pallas kernels for 19% -> 16%
where the time goes in v1:
time: 181 us; the launch traced here: 180 us
  Pallas kernels  74.5 us (41%)
  waiting for transfers between devices  48.7 us (27%)
  starting transfers between devices  36.9 us (20%)
  local copies, waits for them, and re-layouts  8.71 us (5%)
  matrix products  8.02 us (4%)
  other arithmetic  2.35 us (1%)
    pallas_call x1, Pallas kernels, body(): pl.pallas_call(functools.partial(mixer_kernel, heads=heads, slices=slices...  25.2 us
    pallas_call x1, Pallas kernels, body(): back_call(scaled, back_low, pair, token_emit, feat_back, den_rows, moment...  22.6 us
    all_to_all x2, waiting for transfers between devices, exchange_sum(): lax.all_to_all(value.reshape(count, block, value.shape[1]), axes, 0, 0, t...  20.5 us
    ppermute x14, waiting for transfers between devices, swap(): return lax.ppermute(value, axis, [(i, i ^ distance) for i in range(size)])  17 us
    ppermute x14, starting transfers between devices, swap(): return lax.ppermute(value, axis, [(i, i ^ distance) for i in range(size)])  16.2 us
    pallas_call x1, Pallas kernels, body(): pl.pallas_call(functools.partial(front_kernel, heads=heads, slices=slices...  14 us
    all_to_all x2, starting transfers between devices, exchange_sum(): lax.all_to_all(value.reshape(count, block, value.shape[1]), axes, 0, 0, t...  9.37 us
    all_to_all x2, waiting for transfers between devices, gather(): lax.all_to_all(jnp.broadcast_to(value[None], (count,) + value.shape), axe...  6.71 us
  transfers between devices with their start and end apart: 19, of which 13 were waited for; matrix products, arithmetic and copies ran while one was open for 6% of the time, Pallas kernels for 16%

profile of v1, /device:TPU:0, one launch (start us, length us, event | category | flops | bytes accessed | tf_op | source)
XLA Modules:
  0.0 180.2 jit_solution(6293769382399987486)
XLA Ops:
  0.6 1.9 %pack.1 = f32[4,192,256]{2,1,0:T(8,128)} custom-call(bf16[64,256]{1,0:T(8,128)(2,1)} %bitcast.75, bf16[64,256]{1,0:T(8,128)(2,1)} %bitcast.76, f32[1,64]{1,0:T(1,128)} %bitcast.77, f32[2,32,64]{2,1,0:T(8,128)} %energy_ref.1, f32[2,32,32]{2,1,0:T(8,128)} %ask_ref.1, f32[2,32,32]{2,1,0:T(8,128)} %look_ref.1, f32[2,32,32]{2,1,0:T(8,128)} %content_ref.1), custom_call_target="tpu_custom_call" | custom-call | tf_op jit(solution)/shard_map/pack/pallas_call | solution.py:503
  2.5 5.2 %all-to-all-start = ((f32[4,192,256]{2,1,0:T(8,128)}), f32[4,192,256]{2,1,0:T(8,128)S(1)}, u32[]{:S(2)}, u32[]{:S(2)}) async-start(f32[4,192,256]{2,1,0:T(8,128)} %pack.1), calls=%async_computation | async-start | bytes 1572864 | tf_op jit(solution)/shard_map/all_to_all | solution.py:516
  7.7 6.3 %norm.1.s_ref = bf16[8192,256]{1,0:T(8,128)(2,1)} custom-call(s32[1]{0:T(128)} %bitcast.member_ref, bf16[32768,256]{1,0:T(8,128)(2,1)} %x_ref.3, f32[1,256]{1,0:T(1,128)} %bitcast.82), custom_call_target="tpu_custom_call" | custom-call | flops 8589934592 | bytes 16777216 | tf_op jit(solution)/shard_map/norm/pallas_call | solution.py:539
  14.1 4.5 %all-to-all-done = f32[4,192,256]{2,1,0:T(8,128)S(1)} async-done(((f32[4,192,256]{2,1,0:T(8,128)}), f32[4,192,256]{2,1,0:T(8,128)S(1)}, u32[]{:S(2)}, u32[]{:S(2)}) %all-to-all-start) | async-done | bytes 786464 | tf_op jit(solution)/shard_map/all_to_all | solution.py:516
  18.6 0.9 copy-done
  19.4 2.8 %unpack.1 = (bf16[528,512]{1,0:T(8,128)(2,1)}, f32[256,528]{1,0:T(8,128)}, bf16[256,256]{1,0:T(8,128)(2,1)}, bf16[256,256]{1,0:T(8,128)(2,1)}, f32[8,32,32]{2,1,...) custom-call(f32[768,256]{1,0:T(8,128)} %bitcast.69), custom_call_target="tpu_custom_call" | custom-call | tf_op jit(solution)/shard_map/unpack/pallas_call | solution.py:519
  22.3 14.0 %front.1 = (bf16[512,8192]{1,0:T(8,128)(2,1)}, f32[512,256]{1,0:T(8,128)}, f32[40,512]{1,0:T(8,128)}) custom-call(bf16[8192,256]{1,0:T(8,128)(2,1)} %norm.1.s_ref, bf16[528,512]{1,0:T(8,128)(2,1)} %get-tuple-element.38.pair_ref, bf16[256,256]{1,0:T(8,128)(2,1)} %get-tuple-element.39.feat_ref.part_ref), custom_call_target="tpu_custom_call" | custom-call | flops 17179869184 | bytes 33554432 | tf_op jit(solution)/shard_map/front/pallas_call | solution.py:552
  36.4 1.5 collective-permute-done
  37.9 0.9 add.67
  38.8 1.7 collective-permute-start.1
  40.4 2.6 %collective-permute-start.2 = (f32[40,512]{1,0:T(8,128)S(1)}, f32[40,512]{1,0:T(8,128)S(1)}, u32[]{:S(2)}, u32[]{:S(2)}) collective-permute-start(f32[40,512]{1,0:T(8,128)S(1)} %add.67), channel_id=1, source_target_pairs={{0,16},{4,20},{8,24},{12,28},{16,0},{20,4},{24,8},{28,12},{1,17},{... | collective-permute-start | bytes 245768 | tf_op jit(solution)/shard_map/ppermute | solution.py:52
  43.2 0.8 copy.35
  44.0 0.8 copy.34
  44.7 5.2 %collective-permute-done.2 = f32[40,512]{1,0:T(8,128)S(1)} collective-permute-done((f32[40,512]{1,0:T(8,128)S(1)}, f32[40,512]{1,0:T(8,128)S(1)}, u32[]{:S(2)}, u32[]{:S(2)}) %collective-permute-start.2) | collective-permute-done | bytes 81952 | tf_op jit(solution)/shard_map/ppermute | solution.py:52
  49.9 1.5 collective-permute-start.4
  51.4 0.6 collective-permute-start.5
  52.0 1.5 collective-permute-start.6
  53.5 1.2 collective-permute-done.4
  54.7 1.1 collective-permute-done.5
  55.9 1.5 collective-permute-done.6
  57.5 0.4 fusion.20
  57.9 0.4 fusion.21
  58.3 0.4 fusion.22
  58.7 0.6 fusion.2
  59.4 0.4 convolution_convert_fusion.2
  59.9 0.3 mul.100.token_ref
  60.2 1.0 convolution_convert_fusion.1.te_ref
  61.2 25.2 %mixer.1 = (bf16[8192,256]{1,0:T(8,128)(2,1)}, bf16[8192,256]{1,0:T(8,128)(2,1)}, bf16[768,256]{1,0:T(8,128)(2,1)}, f32[8,256]{1,0:T(8,128)}, f32[32,512]{1,0:T(8,128)}) custom-call(s32[1]{0:T(128)} %bitcast.member_ref, bf16[32768,256]{1,0:T(8,128)(2,1)} %x_ref.3, bf16[512,8192]{1,0:T(8,128)(2,1)} %get-tuple-element.40.w_ref, bf16[8192,256]{1,0:T(8,128)(2,1)} %loss_ref.1, ...), custom_call_target="tpu_custom_call" | custom-call | flops 27917287424 | bytes 54525952 | tf_op jit(solution)/shard_map/mixer/pallas_call | solution.py:592
  86.5 1.5 collective-permute-done.7
  87.9 0.8 add.77
  88.8 2.6 %collective-permute-start.10 = (f32[32,512]{1,0:T(8,128)S(1)}, f32[32,512]{1,0:T(8,128)S(1)}, u32[]{:S(2)}, u32[]{:S(2)}) collective-permute-start(f32[32,512]{1,0:T(8,128)S(1)} %add.77), channel_id=1, source_target_pairs={{0,24},{4,28},{8,16},{12,20},{16,8},{20,12},{24,0},{28,4},{1,25},{... | collective-permute-start | bytes 196616 | tf_op jit(solution)/shard_map/ppermute | solution.py:52
  91.4 0.6 collective-permute-start.8
  92.0 1.3 collective-permute-start.9
  93.3 2.3 %collective-permute-done.10 = f32[32,512]{1,0:T(8,128)S(1)} collective-permute-done((f32[32,512]{1,0:T(8,128)S(1)}, f32[32,512]{1,0:T(8,128)S(1)}, u32[]{:S(2)}, u32[]{:S(2)}) %collective-permute-start.10) | collective-permute-done | bytes 65568 | tf_op jit(solution)/shard_map/ppermute | solution.py:52
  95.5 1.9 %collective-permute-done.8 = f32[32,512]{1,0:T(8,128)S(1)} collective-permute-done((f32[32,512]{1,0:T(8,128)S(1)}, f32[32,512]{1,0:T(8,128)S(1)}, u32[]{:S(2)}, u32[]{:S(2)}) %collective-permute-start.8) | collective-permute-done | bytes 65568 | tf_op jit(solution)/shard_map/ppermute | solution.py:52
  97.4 0.9 collective-permute-done.9
  98.4 1.6 collective-permute-start.11
  99.9 0.6 collective-permute-start.12
  100.5 1.4 collective-permute-start.13
  101.9 3.7 %all-to-all-start.1 = ((bf16[32,24,256]{2,1,0:T(8,128)(2,1)}), bf16[32,24,256]{2,1,0:T(8,128)(2,1)S(1)}, u32[]{:S(2)}, u32[]{:S(2)}) async-start(bf16[32,24,256]{2,1,0:T(8,128)(2,1)} %bitcast.71), calls=%async_computation.1 | async-start | bytes 786432 | tf_op jit(solution)/shard_map/all_to_all | solution.py:77
  105.8 0.5 fusion.5
  106.3 0.6 multiply_reduce_fusion
  107.1 0.5 fusion.25
  107.6 0.4 fusion.26
  108.9 0.3 mul.112.num_ref
  109.4 1.0 convolution_convert_fusion.fb_ref
  110.3 8.7 %all-to-all-done.1 = bf16[32,24,256]{2,1,0:T(8,128)(2,1)S(1)} async-done(((bf16[32,24,256]{2,1,0:T(8,128)(2,1)}), bf16[32,24,256]{2,1,0:T(8,128)(2,1)S(1)}, u32[]{:S(2)}, u32[]{:S(2)}) %all-to-all-start.1) | async-done | bytes 393248 | tf_op jit(solution)/shard_map/all_to_all | solution.py:77
  119.2 0.9 broadcast_in_dim.44
  120.1 2.8 %all-to-all-start.2 = ((f32[32,24,256]{2,1,0:T(8,128)}), f32[32,24,256]{2,1,0:T(8,128)S(1)}, u32[]{:S(2)}, u32[]{:S(2)}) async-start(f32[32,24,256]{2,1,0:T(8,128)} %broadcast_in_dim.44), calls=%async_computation.2 | async-start | bytes 1572864 | tf_op jit(solution)/shard_map/all_to_all | solution.py:85
  122.9 0.8 broadcast_in_dim.21.den_ref
  123.8 22.6 %back.1 = bf16[768,256]{1,0:T(8,128)(2,1)} custom-call(bf16[8192,256]{1,0:T(8,128)(2,1)} %norm.1.s_ref, bf16[8192,256]{1,0:T(8,128)(2,1)} %get-tuple-element.46.back_ref, bf16[528,512]{1,0:T(8,128)(2,1)} %get-tuple-element.38.pair_ref, bf16[512,256]{1,0:T(8,128)(2,1)} %convolution_convert_fusion.1.te_ref, bf16[512,256]{1,0:T(8,128)(2,1)} %convolution_convert_fusion.fb_ref, ...), custom_call_target="tpu_custom_call" | custom-call | flops 27917287424 | bytes 54525952 | tf_op jit(solution)/shard_map/back/pallas_call | solution.py:698
  146.4 5.6 %all-to-all-start.3 = ((bf16[32,24,256]{2,1,0:T(8,128)(2,1)}), bf16[32,24,256]{2,1,0:T(8,128)(2,1)S(1)}, u32[]{:S(2)}, u32[]{:S(2)}) async-start(bf16[32,24,256]{2,1,0:T(8,128)(2,1)} %bitcast.72), calls=%async_computation.3 | async-start | bytes 786432 | tf_op jit(solution)/shard_map/all_to_all | solution.py:77
  152.1 0.3 fusion.18
  152.4 0.3 fusion.17
  152.8 0.6 constant_dynamic-slice_fusion
  153.4 0.3 fusion.19
  153.8 11.7 %all-to-all-done.3 = bf16[32,24,256]{2,1,0:T(8,128)(2,1)S(1)} async-done(((bf16[32,24,256]{2,1,0:T(8,128)(2,1)}), bf16[32,24,256]{2,1,0:T(8,128)(2,1)S(1)}, u32[]{:S(2)}, u32[]{:S(2)}) %all-to-all-start.3) | async-done | bytes 393248 | tf_op jit(solution)/shard_map/all_to_all | solution.py:77
  165.6 0.7 broadcast_in_dim.45
  166.3 3.4 %all-to-all-start.4 = ((f32[8,24,256]{2,1,0:T(8,128)}), f32[8,24,256]{2,1,0:T(8,128)S(1)}, u32[]{:S(2)}, u32[]{:S(2)}) async-start(f32[8,24,256]{2,1,0:T(8,128)} %broadcast_in_dim.45), calls=%async_computation.4 | async-start | bytes 393216 | tf_op jit(solution)/shard_map/all_to_all | solution.py:85
  169.7 0.6 constant_dynamic-slice_fusion.2
  170.3 0.9 fusion.23
  171.2 6.7 %all-to-all-done.4 = f32[8,24,256]{2,1,0:T(8,128)S(1)} async-done(((f32[8,24,256]{2,1,0:T(8,128)}), f32[8,24,256]{2,1,0:T(8,128)S(1)}, u32[]{:S(2)}, u32[]{:S(2)}) %all-to-all-start.4) | async-done | bytes 196640 | tf_op jit(solution)/shard_map/all_to_all | solution.py:85
  177.9 0.7 copy-done.3
  178.6 1.6 finish.1
  (52 shorter events, 2.1 us)
Async XLA Ops:
  2.5 16.0 %all-to-all-start = ((f32[4,192,256]{2,1,0:T(8,128)}), f32[4,192,256]{2,1,0:T(8,128)S(1)}, u32[]{:S(2)}, u32[]{:S(2)}) async-start(f32[4,192,256]{2,1,0:T(8,128)} %pack.1), calls=%async_computation | async-start | bytes 1572864 | tf_op jit(solution)/shard_map/all_to_all | solution.py:516
  18.6 0.9 copy-start
  22.2 21.0 %copy-start.8 = (bf16[256,256]{1,0:T(8,128)(2,1)S(1)}, bf16[256,256]{1,0:T(8,128)(2,1)}, u32[]{:S(2)}) copy-start(bf16[256,256]{1,0:T(8,128)(2,1)} %contract_ref.1) | copy-start | bytes 393220
  22.2 21.8 %copy-start.7 = (bf16[256,256]{1,0:T(8,128)(2,1)S(1)}, bf16[256,256]{1,0:T(8,128)(2,1)}, u32[]{:S(2)}) copy-start(bf16[256,256]{1,0:T(8,128)(2,1)} %expand_ref.1) | copy-start | bytes 393220
  22.2 35.3 %copy-start.9 = (f32[8,32,32]{2,1,0:T(8,128)S(1)}, f32[8,32,32]{2,1,0:T(8,128)}, u32[]{:S(2)}) copy-start(f32[8,32,32]{2,1,0:T(8,128)} %get-tuple-element.44) | copy-start | bytes 98308
  22.2 35.7 %copy-start.10 = (f32[8,32,32]{2,1,0:T(8,128)S(1)}, f32[8,32,32]{2,1,0:T(8,128)}, u32[]{:S(2)}) copy-start(f32[8,32,32]{2,1,0:T(8,128)} %get-tuple-element.43) | copy-start | bytes 98308
  22.3 36.1 %copy-start.6 = (f32[8,32,32]{2,1,0:T(8,128)S(1)}, f32[8,32,32]{2,1,0:T(8,128)}, u32[]{:S(2)}) copy-start(f32[8,32,32]{2,1,0:T(8,128)} %get-tuple-element.42) | copy-start | bytes 98308
  36.3 23.9 %copy-start.4 = (bf16[256,256]{1,0:T(8,128)(2,1)S(1)}, bf16[256,256]{1,0:T(8,128)(2,1)}, u32[]{:S(2)}) copy-start(bf16[256,256]{1,0:T(8,128)(2,1)} %emit_ref.1) | copy-start | bytes 393220
  36.3 1.6 collective-permute-start
  38.8 6.0 %collective-permute-start.1 = (f32[40,512]{1,0:T(8,128)S(1)}, f32[40,512]{1,0:T(8,128)S(1)}, u32[]{:S(2)}, u32[]{:S(2)}) collective-permute-start(f32[40,512]{1,0:T(8,128)S(1)} %add.67), channel_id=1, source_target_pairs={{0,8},{4,12},{8,0},{12,4},{16,24},{20,28},{24,16},{28,20},{1,9},{5... | collective-permute-start | bytes 245768 | tf_op jit(solution)/shard_map/ppermute | solution.py:52
  40.4 9.5 %collective-permute-start.2 = (f32[40,512]{1,0:T(8,128)S(1)}, f32[40,512]{1,0:T(8,128)S(1)}, u32[]{:S(2)}, u32[]{:S(2)}) collective-permute-start(f32[40,512]{1,0:T(8,128)S(1)} %add.67), channel_id=1, source_target_pairs={{0,16},{4,20},{8,24},{12,28},{16,0},{20,4},{24,8},{28,12},{1,17},{... | collective-permute-start | bytes 245768 | tf_op jit(solution)/shard_map/ppermute | solution.py:52
  43.0 6.9 %collective-permute-start.3 = (f32[40,512]{1,0:T(8,128)S(1)}, f32[40,512]{1,0:T(8,128)S(1)}, u32[]{:S(2)}, u32[]{:S(2)}) collective-permute-start(f32[40,512]{1,0:T(8,128)S(1)} %add.67), channel_id=1, source_target_pairs={{0,24},{4,28},{8,16},{12,20},{16,8},{20,12},{24,0},{28,4},{1,25},{... | collective-permute-start | bytes 245768 | tf_op jit(solution)/shard_map/ppermute | solution.py:52
  49.9 4.8 %collective-permute-start.4 = (f32[40,512]{1,0:T(8,128)S(1)}, f32[40,512]{1,0:T(8,128)S(1)}, u32[]{:S(2)}, u32[]{:S(2)}) collective-permute-start(f32[40,512]{1,0:T(8,128)S(1)} %add_add_fusion.1), channel_id=1, source_target_pairs={{0,1},{1,0},{2,3},{3,2},{4,5},{5,4},{6,7},{7,6},{8,9},{9,8},{10,11... | collective-permute-start | bytes 245768 | tf_op jit(solution)/shard_map/ppermute | solution.py:52
  51.4 4.4 %collective-permute-start.5 = (f32[40,512]{1,0:T(8,128)S(1)}, f32[40,512]{1,0:T(8,128)S(1)}, u32[]{:S(2)}, u32[]{:S(2)}) collective-permute-start(f32[40,512]{1,0:T(8,128)S(1)} %add_add_fusion.1), channel_id=1, source_target_pairs={{0,2},{1,3},{2,0},{3,1},{4,6},{5,7},{6,4},{7,5},{8,10},{9,11},{10,... | collective-permute-start | bytes 245768 | tf_op jit(solution)/shard_map/ppermute | solution.py:52
  52.0 5.3 %collective-permute-start.6 = (f32[40,512]{1,0:T(8,128)S(1)}, f32[40,512]{1,0:T(8,128)S(1)}, u32[]{:S(2)}, u32[]{:S(2)}) collective-permute-start(f32[40,512]{1,0:T(8,128)S(1)} %add_add_fusion.1), channel_id=1, source_target_pairs={{0,3},{1,2},{2,1},{3,0},{4,7},{5,6},{6,5},{7,4},{8,11},{9,10},{10,... | collective-permute-start | bytes 245768 | tf_op jit(solution)/shard_map/ppermute | solution.py:52
  60.2 1.0 copy-start.2
  86.4 1.5 collective-permute-start.7
  88.8 20.6 %copy-start.5 = (bf16[256,256]{1,0:T(8,128)(2,1)S(1)}, bf16[256,256]{1,0:T(8,128)(2,1)}, u32[]{:S(2)}) copy-start(bf16[256,256]{1,0:T(8,128)(2,1)} %get-tuple-element.39.feat_ref.part_ref) | copy-start | bytes 393220
  88.8 6.7 %collective-permute-start.10 = (f32[32,512]{1,0:T(8,128)S(1)}, f32[32,512]{1,0:T(8,128)S(1)}, u32[]{:S(2)}, u32[]{:S(2)}) collective-permute-start(f32[32,512]{1,0:T(8,128)S(1)} %add.77), channel_id=1, source_target_pairs={{0,24},{4,28},{8,16},{12,20},{16,8},{20,12},{24,0},{28,4},{1,25},{... | collective-permute-start | bytes 196616 | tf_op jit(solution)/shard_map/ppermute | solution.py:52
  91.4 6.0 %collective-permute-start.8 = (f32[32,512]{1,0:T(8,128)S(1)}, f32[32,512]{1,0:T(8,128)S(1)}, u32[]{:S(2)}, u32[]{:S(2)}) collective-permute-start(f32[32,512]{1,0:T(8,128)S(1)} %add.77), channel_id=1, source_target_pairs={{0,8},{4,12},{8,0},{12,4},{16,24},{20,28},{24,16},{28,20},{1,9},{5... | collective-permute-start | bytes 196616 | tf_op jit(solution)/shard_map/ppermute | solution.py:52
  92.0 6.4 %collective-permute-start.9 = (f32[32,512]{1,0:T(8,128)S(1)}, f32[32,512]{1,0:T(8,128)S(1)}, u32[]{:S(2)}, u32[]{:S(2)}) collective-permute-start(f32[32,512]{1,0:T(8,128)S(1)} %add.77), channel_id=1, source_target_pairs={{0,16},{4,20},{8,24},{12,28},{16,0},{20,4},{24,8},{28,12},{1,17},{... | collective-permute-start | bytes 196616 | tf_op jit(solution)/shard_map/ppermute | solution.py:52
  98.4 7.3 %collective-permute-start.11 = (f32[32,512]{1,0:T(8,128)S(1)}, f32[32,512]{1,0:T(8,128)S(1)}, u32[]{:S(2)}, u32[]{:S(2)}) collective-permute-start(f32[32,512]{1,0:T(8,128)S(1)} %add_add_fusion.3), channel_id=1, source_target_pairs={{0,1},{1,0},{2,3},{3,2},{4,5},{5,4},{6,7},{7,6},{8,9},{9,8},{10,11... | collective-permute-start | bytes 196616 | tf_op jit(solution)/shard_map/ppermute | solution.py:52
  99.9 5.7 %collective-permute-start.12 = (f32[32,512]{1,0:T(8,128)S(1)}, f32[32,512]{1,0:T(8,128)S(1)}, u32[]{:S(2)}, u32[]{:S(2)}) collective-permute-start(f32[32,512]{1,0:T(8,128)S(1)} %add_add_fusion.3), channel_id=1, source_target_pairs={{0,2},{1,3},{2,0},{3,1},{4,6},{5,7},{6,4},{7,5},{8,10},{9,11},{10,... | collective-permute-start | bytes 196616 | tf_op jit(solution)/shard_map/ppermute | solution.py:52
  100.5 5.2 %collective-permute-start.13 = (f32[32,512]{1,0:T(8,128)S(1)}, f32[32,512]{1,0:T(8,128)S(1)}, u32[]{:S(2)}, u32[]{:S(2)}) collective-permute-start(f32[32,512]{1,0:T(8,128)S(1)} %add_add_fusion.3), channel_id=1, source_target_pairs={{0,3},{1,2},{2,1},{3,0},{4,7},{5,6},{6,5},{7,4},{8,11},{9,10},{10,... | collective-permute-start | bytes 196616 | tf_op jit(solution)/shard_map/ppermute | solution.py:52
  101.9 17.2 %all-to-all-start.1 = ((bf16[32,24,256]{2,1,0:T(8,128)(2,1)}), bf16[32,24,256]{2,1,0:T(8,128)(2,1)S(1)}, u32[]{:S(2)}, u32[]{:S(2)}) async-start(bf16[32,24,256]{2,1,0:T(8,128)(2,1)} %bitcast.71), calls=%async_computation.1 | async-start | bytes 786432 | tf_op jit(solution)/shard_map/all_to_all | solution.py:77
  109.3 14.5 %copy-start.1 = (bf16[256,512]{1,0:T(8,128)(2,1)}, bf16[256,512]{1,0:T(8,128)(2,1)S(1)}, u32[]{:S(2)}) copy-start(bf16[256,512]{1,0:T(8,128)(2,1)S(1)} %mul.112.num_ref) | copy-start | bytes 786436
  120.1 26.3 %all-to-all-start.2 = ((f32[32,24,256]{2,1,0:T(8,128)}), f32[32,24,256]{2,1,0:T(8,128)S(1)}, u32[]{:S(2)}, u32[]{:S(2)}) async-start(f32[32,24,256]{2,1,0:T(8,128)} %broadcast_in_dim.44), calls=%async_computation.2 | async-start | bytes 1572864 | tf_op jit(solution)/shard_map/all_to_all | solution.py:85
  146.4 19.1 %all-to-all-start.3 = ((bf16[32,24,256]{2,1,0:T(8,128)(2,1)}), bf16[32,24,256]{2,1,0:T(8,128)(2,1)S(1)}, u32[]{:S(2)}, u32[]{:S(2)}) async-start(bf16[32,24,256]{2,1,0:T(8,128)(2,1)} %bitcast.72), calls=%async_computation.3 | async-start | bytes 786432 | tf_op jit(solution)/shard_map/all_to_all | solution.py:77
  166.3 11.6 %all-to-all-start.4 = ((f32[8,24,256]{2,1,0:T(8,128)}), f32[8,24,256]{2,1,0:T(8,128)S(1)}, u32[]{:S(2)}, u32[]{:S(2)}) async-start(f32[8,24,256]{2,1,0:T(8,128)} %broadcast_in_dim.45), calls=%async_computation.4 | async-start | bytes 393216 | tf_op jit(solution)/shard_map/all_to_all | solution.py:85
  177.9 0.7 copy-start.3

commit v2 on v1

--- a/solution.py
+++ b/solution.py
@@ -154,7 +154,8 @@
         content_ref[h] = rest[:, slices + 2 * channels : slices + 3 * channels]
         spot = slices + 3 * channels
         energy_ref[own, lanes + h : lanes + h + 1] = rest[:, spot : spot + 1]
-    logits_of = dot(energy_ref[...], div_ref[...].astype(jnp.float32), TN, HIGHEST)
+    energy_high, energy_low = halves(energy_ref[...])
+    logits_of = dot(energy_high, div_ref[...], TN) + dot(energy_low, div_ref[...], TN)
     pair_ref[...] = jnp.concatenate(halves(logits_of), axis=1)
 
 
@@ -246,7 +247,6 @@
     x_ref,
     w_ref,
     loss_ref,
-    te_ref,
     gain_ref,
     expand_ref,
     expand_t_ref,
@@ -260,6 +260,7 @@
     grads_ref,
     gains_ref,
     tg_ref,
+    te_ref,
     acc_scr,
     wr_scr,
     gain_scr,
@@ -272,6 +273,7 @@
 
     @pl.when(step == 0)
     def _():
+        te_ref[...] = dot(token_ref[...], emit_ref[...], TN).astype(jnp.bfloat16)
         acc_scr[...] = jnp.zeros_like(acc_scr)
         gain_scr[...] = jnp.zeros_like(gain_scr)
         wr_scr[...] = jnp.zeros_like(wr_scr)
@@ -326,7 +328,6 @@
     back_ref,
     pair_ref,
     te_ref,
-    fb_ref,
     den_ref,
     m_ref,
     energy_ref,
@@ -341,6 +342,8 @@
     r_scr,
     d_scr,
     g_scr,
+    den_scr,
+    tf_scr,
     *,
     heads,
     slices,
@@ -354,12 +357,15 @@
     @pl.when(step == 0)
     def _():
         g_scr[...] = jnp.zeros_like(g_scr)
-        d_scr[...] = jnp.zeros_like(d_scr)
+        den_scr[...] = jnp.broadcast_to(den_ref[...], den_scr.shape)
+        width = te_ref.shape[1]
+        tf_scr[:, :width] = te_ref[...]
+        tf_scr[:, width:] = dot(num_ref[...], part_ref[...], TN).astype(jnp.bfloat16)
 
     scaled = s_ref[...]
     z_scr[...] = dot(pair_ref[...], jnp.concatenate([scaled, scaled], axis=1), NT)
     b_scr[...] = dot(
-        jnp.concatenate([te_ref[...], fb_ref[...]], axis=1),
+        tf_scr[...],
         jnp.concatenate([back_ref[...], scaled], axis=1),
         NT,
     )
@@ -375,7 +381,7 @@
             bent = jnp.tanh(z)
             raised = jnp.exp(SCORE_LIMIT * bent)
             weights = raised * (1.0 / jnp.sum(raised, axis=0, keepdims=True))
-            back_w = b_scr[span, cols] + jnp.concatenate([den_ref[span, :]] * (chunk // 128), axis=1)
+            back_w = b_scr[span, cols] + jnp.concatenate([den_scr[span, :]] * (chunk // 128), axis=1)
             middle = jnp.sum(weights * back_w, axis=0, keepdims=True)
             q = weights * (back_w - middle) * (1.0 - bent * bent)
             d_scr[span, cols] = (q * inverse).astype(jnp.bfloat16)
@@ -585,11 +591,8 @@
     )
     token_low = token_out.astype(jnp.bfloat16)
     token_rows = block_diagonal(token_low.transpose(0, 2, 1))
-    token_emit = lax.dot_general(
-        token_rows, emit_projection, TN, preferred_element_type=jnp.float32
-    ).astype(jnp.bfloat16)
-
-    block_result, back_low, grads, gains, token_grad = pl.pallas_call(
+
+    block_result, back_low, grads, gains, token_grad, token_emit = pl.pallas_call(
         functools.partial(mixer_kernel, heads=heads, slices=slices),
         grid_spec=pltpu.PrefetchScalarGridSpec(
             num_scalar_prefetch=1,
@@ -598,7 +601,6 @@
                 own_block,
                 column_block,
                 row_block,
-                whole((lanes, width)),
                 whole((1, width)),
                 whole(expand_factor.shape),
                 whole(expand_factor.shape[::-1]),
@@ -614,6 +616,7 @@
                 whole((3 * width, width)),
                 whole((8, width)),
                 whole((channels, lanes)),
+                whole((lanes, width)),
             ],
             scratch_shapes=[
                 pltpu.VMEM((2 * width, width), jnp.float32),
@@ -627,6 +630,7 @@
             jax.ShapeDtypeStruct((3 * width, width), jnp.bfloat16),
             jax.ShapeDtypeStruct((8, width), jnp.float32),
             jax.ShapeDtypeStruct((channels, lanes), jnp.float32),
+            jax.ShapeDtypeStruct((lanes, width), jnp.bfloat16),
         ],
         compiler_params=params(),
         cost_estimate=cost(26, rows, width),
@@ -636,7 +640,6 @@
         mesh_signals,
         weights,
         loss_sensitivity,
-        token_emit,
         premlp_scale[None, :],
         expand_factor,
         expand_factor.T,
@@ -652,14 +655,11 @@
     token_grad = token_grad.reshape(channels, heads, slices).transpose(1, 2, 0)
     back_num, back_den, asking_slope, lookup_slope, content_slope = token_back(token_grad)
     num_low = block_diagonal(back_num.astype(jnp.bfloat16).transpose(0, 2, 1))
-    feat_back = lax.dot_general(
-        num_low, part_t, TN, preferred_element_type=jnp.float32
-    ).astype(jnp.bfloat16)
-    den_rows = jnp.broadcast_to(back_den.reshape(lanes, 1), (lanes, 128))
+    den_rows = back_den.reshape(lanes, 1)
 
     everyone = ("head", "pts")
     grads = exchange_sum(grads, everyone)
-    grads = gather(grads, everyone)
+    grads = gather(grads.astype(jnp.bfloat16), everyone).astype(jnp.float32)
 
     unit = 2 * channels + 16
     grain = 8 * lax.axis_size("pts")
@@ -672,8 +672,7 @@
             row_block,
             whole((total_rows, 2 * width)),
             whole((lanes, width)),
-            whole((lanes, width)),
-            whole((lanes, 128)),
+            whole((lanes, 1)),
             whole((lanes, width)),
             whole((heads * channels, total_rows)),
             whole((heads * channels, lanes)),
@@ -689,6 +688,8 @@
             pltpu.VMEM((heads, tile), jnp.float32),
             pltpu.VMEM((total_rows, tile), jnp.bfloat16),
             pltpu.VMEM((total_rows, width), jnp.float32),
+            pltpu.VMEM((lanes, 128), jnp.float32),
+            pltpu.VMEM((lanes, 2 * width), jnp.bfloat16),
         ],
         out_shape=jax.ShapeDtypeStruct((groups * block, width), jnp.bfloat16),
         compiler_params=params(),
@@ -700,7 +701,6 @@
         back_low,
         pair,
         token_emit,
-        feat_back,
         den_rows,
         moment,
         energy_rows,

time: 181 us -> 180 us (level)
  matrix products: 8.02 us -> 6.07 us
    dot_general x2 -> x0, matrix products: 1.95 us -> none  [the longest x1 0.97 us: body(): lax.dot_general(token_rows, emit_projection, TN, preferred_element_type=j...]
  transfers between devices with their start and end apart: 19 -> 19, of which waited for: 13 -> 13; matrix products, arithmetic and copies ran while one was open for 6% -> 5% of each run, Pallas kernels for 16% -> 16%
where the time goes in v2:
time: 180 us; the launch traced here: 179 us
  Pallas kernels  74.5 us (41%)
  waiting for transfers between devices  48.1 us (27%)
  starting transfers between devices  36.8 us (20%)
  local copies, waits for them, and re-layouts  9.92 us (6%)
  matrix products  6.07 us (3%)
  other arithmetic  2.43 us (1%)
    pallas_call x1, Pallas kernels, body(): pl.pallas_call(functools.partial(mixer_kernel, heads=heads, slices=slices...  25.4 us
    pallas_call x1, Pallas kernels, body(): back_call(scaled, back_low, pair, token_emit, den_rows, moment, energy_ro...  22.4 us
    all_to_all x2, waiting for transfers between devices, exchange_sum(): lax.all_to_all(value.reshape(count, block, value.shape[1]), axes, 0, 0, t...  19.9 us
    ppermute x14, waiting for transfers between devices, swap(): return lax.ppermute(value, axis, [(i, i ^ distance) for i in range(size)])  17 us
    ppermute x14, starting transfers between devices, swap(): return lax.ppermute(value, axis, [(i, i ^ distance) for i in range(size)])  16.1 us
    pallas_call x1, Pallas kernels, body(): pl.pallas_call(functools.partial(front_kernel, heads=heads, slices=slices...  14 us
    all_to_all x2, starting transfers between devices, exchange_sum(): lax.all_to_all(value.reshape(count, block, value.shape[1]), axes, 0, 0, t...  9.35 us
    all_to_all x2, waiting for transfers between devices, gather(): lax.all_to_all(jnp.broadcast_to(value[None], (count,) + value.shape), axe...  6.71 us
  transfers between devices with their start and end apart: 19, of which 13 were waited for; matrix products, arithmetic and copies ran while one was open for 5% of the time, Pallas kernels for 16%

profile of v2, /device:TPU:0, one launch (start us, length us, event | category | flops | bytes accessed | tf_op | source)
XLA Modules:
  0.0 178.8 jit_solution(66457458842196090)
XLA Ops:
  0.6 1.9 %pack.1 = f32[4,192,256]{2,1,0:T(8,128)} custom-call(bf16[64,256]{1,0:T(8,128)(2,1)} %bitcast.72, bf16[64,256]{1,0:T(8,128)(2,1)} %bitcast.73, f32[1,64]{1,0:T(1,128)} %bitcast.74, f32[2,32,64]{2,1,0:T(8,128)} %energy_ref.1, f32[2,32,32]{2,1,0:T(8,128)} %ask_ref.1, f32[2,32,32]{2,1,0:T(8,128)} %look_ref.1, f32[2,32,32]{2,1,0:T(8,128)} %content_ref.1), custom_call_target="tpu_custom_call" | custom-call | tf_op jit(solution)/shard_map/pack/pallas_call | solution.py:509
  2.5 5.2 %all-to-all-start = ((f32[4,192,256]{2,1,0:T(8,128)}), f32[4,192,256]{2,1,0:T(8,128)S(1)}, u32[]{:S(2)}, u32[]{:S(2)}) async-start(f32[4,192,256]{2,1,0:T(8,128)} %pack.1), calls=%async_computation | async-start | bytes 1572864 | tf_op jit(solution)/shard_map/all_to_all | solution.py:522
  7.7 6.3 %norm.1.s_ref = bf16[8192,256]{1,0:T(8,128)(2,1)} custom-call(s32[1]{0:T(128)} %bitcast.member_ref, bf16[32768,256]{1,0:T(8,128)(2,1)} %x_ref.3, f32[1,256]{1,0:T(1,128)} %bitcast.79), custom_call_target="tpu_custom_call" | custom-call | flops 8589934592 | bytes 16777216 | tf_op jit(solution)/shard_map/norm/pallas_call | solution.py:545
  14.1 4.5 %all-to-all-done = f32[4,192,256]{2,1,0:T(8,128)S(1)} async-done(((f32[4,192,256]{2,1,0:T(8,128)}), f32[4,192,256]{2,1,0:T(8,128)S(1)}, u32[]{:S(2)}, u32[]{:S(2)}) %all-to-all-start) | async-done | bytes 786464 | tf_op jit(solution)/shard_map/all_to_all | solution.py:522
  18.6 0.9 copy-done
  19.4 2.7 %unpack.1 = (bf16[528,512]{1,0:T(8,128)(2,1)}, f32[256,528]{1,0:T(8,128)}, bf16[256,256]{1,0:T(8,128)(2,1)}, bf16[256,256]{1,0:T(8,128)(2,1)}, f32[8,32,32]{2,1,...) custom-call(f32[768,256]{1,0:T(8,128)} %bitcast.66), custom_call_target="tpu_custom_call" | custom-call | tf_op jit(solution)/shard_map/unpack/pallas_call | solution.py:525
  22.2 14.0 %front.1 = (bf16[512,8192]{1,0:T(8,128)(2,1)}, f32[512,256]{1,0:T(8,128)}, f32[40,512]{1,0:T(8,128)}) custom-call(bf16[8192,256]{1,0:T(8,128)(2,1)} %norm.1.s_ref, bf16[528,512]{1,0:T(8,128)(2,1)} %get-tuple-element.39.pair_ref, bf16[256,256]{1,0:T(8,128)(2,1)} %get-tuple-element.40.feat_ref.part_ref), custom_call_target="tpu_custom_call" | custom-call | flops 17179869184 | bytes 33554432 | tf_op jit(solution)/shard_map/front/pallas_call | solution.py:558
  36.2 1.5 collective-permute-done
  37.7 0.9 add.67
  38.6 1.7 collective-permute-start.1
  40.3 2.6 %collective-permute-start.2 = (f32[40,512]{1,0:T(8,128)S(1)}, f32[40,512]{1,0:T(8,128)S(1)}, u32[]{:S(2)}, u32[]{:S(2)}) collective-permute-start(f32[40,512]{1,0:T(8,128)S(1)} %add.67), channel_id=1, source_target_pairs={{0,16},{4,20},{8,24},{12,28},{16,0},{20,4},{24,8},{28,12},{1,17},{... | collective-permute-start | bytes 245768 | tf_op jit(solution)/shard_map/ppermute | solution.py:52
  43.1 0.8 copy.40
  43.8 0.8 copy.41
  44.6 5.2 %collective-permute-done.2 = f32[40,512]{1,0:T(8,128)S(1)} collective-permute-done((f32[40,512]{1,0:T(8,128)S(1)}, f32[40,512]{1,0:T(8,128)S(1)}, u32[]{:S(2)}, u32[]{:S(2)}) %collective-permute-start.2) | collective-permute-done | bytes 81952 | tf_op jit(solution)/shard_map/ppermute | solution.py:52
  49.8 1.5 collective-permute-start.4
  51.3 0.6 collective-permute-start.5
  51.8 1.5 collective-permute-start.6
  53.3 1.2 collective-permute-done.4
  54.6 1.1 collective-permute-done.5
  55.7 1.5 collective-permute-done.6
  57.4 0.4 fusion.20
  57.8 0.4 fusion.21
  58.2 0.4 fusion.22
  58.6 0.6 fusion.2
  59.2 0.4 convolution_convert_fusion
  59.7 1.0 mul.100.token_ref
  60.8 25.4 %mixer.1 = (bf16[8192,256]{1,0:T(8,128)(2,1)}, bf16[8192,256]{1,0:T(8,128)(2,1)}, bf16[768,256]{1,0:T(8,128)(2,1)}, f32[8,256]{1,0:T(8,128)}, f32[32,512]{1,0:T(8,128)}, /*index=5*/bf16[512,256]{1,0:T(8,128)(2,1)}) custom-call(s32[1]{0:T(128)} %bitcast.member_ref, bf16[32768,256]{1,0:T(8,128)(2,1)} %x_ref.3, bf16[512,8192]{1,0:T(8,128)(2,1)} %get-tuple-element.41.w_ref, ...), custom_call_target="tpu_custom_call" | custom-call | flops 27917287424 | bytes 54525952 | tf_op jit(solution)/shard_map/mixer/pallas_call | solution.py:595
  86.3 1.5 collective-permute-done.7
  87.7 0.8 add.77
  88.6 2.6 %collective-permute-start.10 = (f32[32,512]{1,0:T(8,128)S(1)}, f32[32,512]{1,0:T(8,128)S(1)}, u32[]{:S(2)}, u32[]{:S(2)}) collective-permute-start(f32[32,512]{1,0:T(8,128)S(1)} %add.77), channel_id=1, source_target_pairs={{0,24},{4,28},{8,16},{12,20},{16,8},{20,12},{24,0},{28,4},{1,25},{... | collective-permute-start | bytes 196616 | tf_op jit(solution)/shard_map/ppermute | solution.py:52
  91.2 0.5 collective-permute-start.8
  91.7 1.3 collective-permute-start.9
  93.0 2.3 %collective-permute-done.10 = f32[32,512]{1,0:T(8,128)S(1)} collective-permute-done((f32[32,512]{1,0:T(8,128)S(1)}, f32[32,512]{1,0:T(8,128)S(1)}, u32[]{:S(2)}, u32[]{:S(2)}) %collective-permute-start.10) | collective-permute-done | bytes 65568 | tf_op jit(solution)/shard_map/ppermute | solution.py:52
  95.3 1.9 %collective-permute-done.8 = f32[32,512]{1,0:T(8,128)S(1)} collective-permute-done((f32[32,512]{1,0:T(8,128)S(1)}, f32[32,512]{1,0:T(8,128)S(1)}, u32[]{:S(2)}, u32[]{:S(2)}) %collective-permute-start.8) | collective-permute-done | bytes 65568 | tf_op jit(solution)/shard_map/ppermute | solution.py:52
  97.2 0.9 collective-permute-done.9
  98.1 1.6 collective-permute-start.11
  99.7 0.6 collective-permute-start.12
  100.3 1.4 collective-permute-start.13
  101.7 3.7 %all-to-all-start.1 = ((bf16[32,24,256]{2,1,0:T(8,128)(2,1)}), bf16[32,24,256]{2,1,0:T(8,128)(2,1)S(1)}, u32[]{:S(2)}, u32[]{:S(2)}) async-start(bf16[32,24,256]{2,1,0:T(8,128)(2,1)} %bitcast.68), calls=%async_computation.1 | async-start | bytes 786432 | tf_op jit(solution)/shard_map/all_to_all | solution.py:77
  105.6 0.5 fusion.5
  106.1 0.6 multiply_reduce_fusion
  106.9 0.5 fusion.25
  107.4 0.4 fusion.26
  108.0 0.3 convolution_add_fusion.1
  108.3 0.3 fusion.12
  108.7 1.0 mul.116.num_ref
  109.7 0.9 neg.24.den_ref
  110.7 8.2 %all-to-all-done.1 = bf16[32,24,256]{2,1,0:T(8,128)(2,1)S(1)} async-done(((bf16[32,24,256]{2,1,0:T(8,128)(2,1)}), bf16[32,24,256]{2,1,0:T(8,128)(2,1)S(1)}, u32[]{:S(2)}, u32[]{:S(2)}) %all-to-all-start.1) | async-done | bytes 393248 | tf_op jit(solution)/shard_map/all_to_all | solution.py:77
  118.9 0.8 broadcast_in_dim.38
  119.7 2.8 %all-to-all-start.2 = ((bf16[32,24,256]{2,1,0:T(8,128)(2,1)}), bf16[32,24,256]{2,1,0:T(8,128)(2,1)S(1)}, u32[]{:S(2)}, u32[]{:S(2)}) async-start(bf16[32,24,256]{2,1,0:T(8,128)(2,1)} %broadcast_in_dim.38), calls=%async_computation.2 | async-start | bytes 786432 | tf_op jit(solution)/shard_map/all_to_all | solution.py:85
  122.5 22.4 %back.1 = bf16[768,256]{1,0:T(8,128)(2,1)} custom-call(bf16[8192,256]{1,0:T(8,128)(2,1)} %norm.1.s_ref, bf16[8192,256]{1,0:T(8,128)(2,1)} %get-tuple-element.47.back_ref, bf16[528,512]{1,0:T(8,128)(2,1)} %get-tuple-element.39.pair_ref, bf16[512,256]{1,0:T(8,128)(2,1)} %get-tuple-element.48.te_ref, f32[512,1]{1,0:T(8,128)} %neg.24.den_ref, ...), custom_call_target="tpu_custom_call" | custom-call | flops 27917287424 | bytes 54525952 | tf_op jit(solution)/shard_map/back/pallas_call | solution.py:699
  145.0 5.6 %all-to-all-start.3 = ((bf16[32,24,256]{2,1,0:T(8,128)(2,1)}), bf16[32,24,256]{2,1,0:T(8,128)(2,1)S(1)}, u32[]{:S(2)}, u32[]{:S(2)}) async-start(bf16[32,24,256]{2,1,0:T(8,128)(2,1)} %bitcast.69), calls=%async_computation.3 | async-start | bytes 786432 | tf_op jit(solution)/shard_map/all_to_all | solution.py:77
  150.7 0.3 fusion.18
  151.0 0.3 fusion.17
  151.4 0.6 constant_dynamic-slice_fusion
  152.0 0.3 fusion.19
  152.4 11.7 %all-to-all-done.3 = bf16[32,24,256]{2,1,0:T(8,128)(2,1)S(1)} async-done(((bf16[32,24,256]{2,1,0:T(8,128)(2,1)}), bf16[32,24,256]{2,1,0:T(8,128)(2,1)S(1)}, u32[]{:S(2)}, u32[]{:S(2)}) %all-to-all-start.3) | async-done | bytes 393248 | tf_op jit(solution)/shard_map/all_to_all | solution.py:77
  164.2 0.7 broadcast_in_dim.39
  164.9 3.4 %all-to-all-start.4 = ((f32[8,24,256]{2,1,0:T(8,128)}), f32[8,24,256]{2,1,0:T(8,128)S(1)}, u32[]{:S(2)}, u32[]{:S(2)}) async-start(f32[8,24,256]{2,1,0:T(8,128)} %broadcast_in_dim.39), calls=%async_computation.4 | async-start | bytes 393216 | tf_op jit(solution)/shard_map/all_to_all | solution.py:85
  168.3 0.6 constant_dynamic-slice_fusion.2
  168.9 0.9 fusion.23
  169.8 6.7 %all-to-all-done.4 = f32[8,24,256]{2,1,0:T(8,128)S(1)} async-done(((f32[8,24,256]{2,1,0:T(8,128)}), f32[8,24,256]{2,1,0:T(8,128)S(1)}, u32[]{:S(2)}, u32[]{:S(2)}) %all-to-all-start.4) | async-done | bytes 196640 | tf_op jit(solution)/shard_map/all_to_all | solution.py:85
  176.5 0.7 copy-done.1
  177.2 1.6 finish.1
  (42 shorter events, 1.5 us)
Async XLA Ops:
  2.5 16.0 %all-to-all-start = ((f32[4,192,256]{2,1,0:T(8,128)}), f32[4,192,256]{2,1,0:T(8,128)S(1)}, u32[]{:S(2)}, u32[]{:S(2)}) async-start(f32[4,192,256]{2,1,0:T(8,128)} %pack.1), calls=%async_computation | async-start | bytes 1572864 | tf_op jit(solution)/shard_map/all_to_all | solution.py:522
  18.6 0.9 copy-start
  22.1 20.9 %copy-start.3 = (bf16[256,256]{1,0:T(8,128)(2,1)S(1)}, bf16[256,256]{1,0:T(8,128)(2,1)}, u32[]{:S(2)}) copy-start(bf16[256,256]{1,0:T(8,128)(2,1)} %expand_ref.1) | copy-start | bytes 393220
  22.1 21.7 %copy-start.4 = (bf16[256,256]{1,0:T(8,128)(2,1)S(1)}, bf16[256,256]{1,0:T(8,128)(2,1)}, u32[]{:S(2)}) copy-start(bf16[256,256]{1,0:T(8,128)(2,1)} %contract_ref.1) | copy-start | bytes 393220
  22.1 35.2 %copy-start.5 = (f32[8,32,32]{2,1,0:T(8,128)S(1)}, f32[8,32,32]{2,1,0:T(8,128)}, u32[]{:S(2)}) copy-start(f32[8,32,32]{2,1,0:T(8,128)} %get-tuple-element.45) | copy-start | bytes 98308
  22.2 35.6 %copy-start.6 = (f32[8,32,32]{2,1,0:T(8,128)S(1)}, f32[8,32,32]{2,1,0:T(8,128)}, u32[]{:S(2)}) copy-start(f32[8,32,32]{2,1,0:T(8,128)} %get-tuple-element.44) | copy-start | bytes 98308
  22.2 36.0 %copy-start.2 = (f32[8,32,32]{2,1,0:T(8,128)S(1)}, f32[8,32,32]{2,1,0:T(8,128)}, u32[]{:S(2)}) copy-start(f32[8,32,32]{2,1,0:T(8,128)} %get-tuple-element.43) | copy-start | bytes 98308
  36.2 1.5 collective-permute-start
  38.6 6.0 %collective-permute-start.1 = (f32[40,512]{1,0:T(8,128)S(1)}, f32[40,512]{1,0:T(8,128)S(1)}, u32[]{:S(2)}, u32[]{:S(2)}) collective-permute-start(f32[40,512]{1,0:T(8,128)S(1)} %add.67), channel_id=1, source_target_pairs={{0,8},{4,12},{8,0},{12,4},{16,24},{20,28},{24,16},{28,20},{1,9},{5... | collective-permute-start | bytes 245768 | tf_op jit(solution)/shard_map/ppermute | solution.py:52
  40.3 9.5 %collective-permute-start.2 = (f32[40,512]{1,0:T(8,128)S(1)}, f32[40,512]{1,0:T(8,128)S(1)}, u32[]{:S(2)}, u32[]{:S(2)}) collective-permute-start(f32[40,512]{1,0:T(8,128)S(1)} %add.67), channel_id=1, source_target_pairs={{0,16},{4,20},{8,24},{12,28},{16,0},{20,4},{24,8},{28,12},{1,17},{... | collective-permute-start | bytes 245768 | tf_op jit(solution)/shard_map/ppermute | solution.py:52
  42.9 6.9 %collective-permute-start.3 = (f32[40,512]{1,0:T(8,128)S(1)}, f32[40,512]{1,0:T(8,128)S(1)}, u32[]{:S(2)}, u32[]{:S(2)}) collective-permute-start(f32[40,512]{1,0:T(8,128)S(1)} %add.67), channel_id=1, source_target_pairs={{0,24},{4,28},{8,16},{12,20},{16,8},{20,12},{24,0},{28,4},{1,25},{... | collective-permute-start | bytes 245768 | tf_op jit(solution)/shard_map/ppermute | solution.py:52
  49.8 4.8 %collective-permute-start.4 = (f32[40,512]{1,0:T(8,128)S(1)}, f32[40,512]{1,0:T(8,128)S(1)}, u32[]{:S(2)}, u32[]{:S(2)}) collective-permute-start(f32[40,512]{1,0:T(8,128)S(1)} %add_add_fusion.1), channel_id=1, source_target_pairs={{0,1},{1,0},{2,3},{3,2},{4,5},{5,4},{6,7},{7,6},{8,9},{9,8},{10,11... | collective-permute-start | bytes 245768 | tf_op jit(solution)/shard_map/ppermute | solution.py:52
  51.3 4.4 %collective-permute-start.5 = (f32[40,512]{1,0:T(8,128)S(1)}, f32[40,512]{1,0:T(8,128)S(1)}, u32[]{:S(2)}, u32[]{:S(2)}) collective-permute-start(f32[40,512]{1,0:T(8,128)S(1)} %add_add_fusion.1), channel_id=1, source_target_pairs={{0,2},{1,3},{2,0},{3,1},{4,6},{5,7},{6,4},{7,5},{8,10},{9,11},{10,... | collective-permute-start | bytes 245768 | tf_op jit(solution)/shard_map/ppermute | solution.py:52
  51.8 5.3 %collective-permute-start.6 = (f32[40,512]{1,0:T(8,128)S(1)}, f32[40,512]{1,0:T(8,128)S(1)}, u32[]{:S(2)}, u32[]{:S(2)}) collective-permute-start(f32[40,512]{1,0:T(8,128)S(1)} %add_add_fusion.1), channel_id=1, source_target_pairs={{0,3},{1,2},{2,1},{3,0},{4,7},{5,6},{6,5},{7,4},{8,11},{9,10},{10,... | collective-permute-start | bytes 245768 | tf_op jit(solution)/shard_map/ppermute | solution.py:52
  86.2 1.5 collective-permute-start.7
  88.6 6.7 %collective-permute-start.10 = (f32[32,512]{1,0:T(8,128)S(1)}, f32[32,512]{1,0:T(8,128)S(1)}, u32[]{:S(2)}, u32[]{:S(2)}) collective-permute-start(f32[32,512]{1,0:T(8,128)S(1)} %add.77), channel_id=1, source_target_pairs={{0,24},{4,28},{8,16},{12,20},{16,8},{20,12},{24,0},{28,4},{1,25},{... | collective-permute-start | bytes 196616 | tf_op jit(solution)/shard_map/ppermute | solution.py:52
  91.2 6.0 %collective-permute-start.8 = (f32[32,512]{1,0:T(8,128)S(1)}, f32[32,512]{1,0:T(8,128)S(1)}, u32[]{:S(2)}, u32[]{:S(2)}) collective-permute-start(f32[32,512]{1,0:T(8,128)S(1)} %add.77), channel_id=1, source_target_pairs={{0,8},{4,12},{8,0},{12,4},{16,24},{20,28},{24,16},{28,20},{1,9},{5... | collective-permute-start | bytes 196616 | tf_op jit(solution)/shard_map/ppermute | solution.py:52
  91.7 6.4 %collective-permute-start.9 = (f32[32,512]{1,0:T(8,128)S(1)}, f32[32,512]{1,0:T(8,128)S(1)}, u32[]{:S(2)}, u32[]{:S(2)}) collective-permute-start(f32[32,512]{1,0:T(8,128)S(1)} %add.77), channel_id=1, source_target_pairs={{0,16},{4,20},{8,24},{12,28},{16,0},{20,4},{24,8},{28,12},{1,17},{... | collective-permute-start | bytes 196616 | tf_op jit(solution)/shard_map/ppermute | solution.py:52
  98.1 7.3 %collective-permute-start.11 = (f32[32,512]{1,0:T(8,128)S(1)}, f32[32,512]{1,0:T(8,128)S(1)}, u32[]{:S(2)}, u32[]{:S(2)}) collective-permute-start(f32[32,512]{1,0:T(8,128)S(1)} %add_add_fusion.3), channel_id=1, source_target_pairs={{0,1},{1,0},{2,3},{3,2},{4,5},{5,4},{6,7},{7,6},{8,9},{9,8},{10,11... | collective-permute-start | bytes 196616 | tf_op jit(solution)/shard_map/ppermute | solution.py:52
  99.7 5.7 %collective-permute-start.12 = (f32[32,512]{1,0:T(8,128)S(1)}, f32[32,512]{1,0:T(8,128)S(1)}, u32[]{:S(2)}, u32[]{:S(2)}) collective-permute-start(f32[32,512]{1,0:T(8,128)S(1)} %add_add_fusion.3), channel_id=1, source_target_pairs={{0,2},{1,3},{2,0},{3,1},{4,6},{5,7},{6,4},{7,5},{8,10},{9,11},{10,... | collective-permute-start | bytes 196616 | tf_op jit(solution)/shard_map/ppermute | solution.py:52
  100.3 5.2 %collective-permute-start.13 = (f32[32,512]{1,0:T(8,128)S(1)}, f32[32,512]{1,0:T(8,128)S(1)}, u32[]{:S(2)}, u32[]{:S(2)}) collective-permute-start(f32[32,512]{1,0:T(8,128)S(1)} %add_add_fusion.3), channel_id=1, source_target_pairs={{0,3},{1,2},{2,1},{3,0},{4,7},{5,6},{6,5},{7,4},{8,11},{9,10},{10,... | collective-permute-start | bytes 196616 | tf_op jit(solution)/shard_map/ppermute | solution.py:52
  101.7 17.2 %all-to-all-start.1 = ((bf16[32,24,256]{2,1,0:T(8,128)(2,1)}), bf16[32,24,256]{2,1,0:T(8,128)(2,1)S(1)}, u32[]{:S(2)}, u32[]{:S(2)}) async-start(bf16[32,24,256]{2,1,0:T(8,128)(2,1)} %bitcast.68), calls=%async_computation.1 | async-start | bytes 786432 | tf_op jit(solution)/shard_map/all_to_all | solution.py:77
  119.7 25.3 %all-to-all-start.2 = ((bf16[32,24,256]{2,1,0:T(8,128)(2,1)}), bf16[32,24,256]{2,1,0:T(8,128)(2,1)S(1)}, u32[]{:S(2)}, u32[]{:S(2)}) async-start(bf16[32,24,256]{2,1,0:T(8,128)(2,1)} %broadcast_in_dim.38), calls=%async_computation.2 | async-start | bytes 786432 | tf_op jit(solution)/shard_map/all_to_all | solution.py:85
  145.0 19.1 %all-to-all-start.3 = ((bf16[32,24,256]{2,1,0:T(8,128)(2,1)}), bf16[32,24,256]{2,1,0:T(8,128)(2,1)S(1)}, u32[]{:S(2)}, u32[]{:S(2)}) async-start(bf16[32,24,256]{2,1,0:T(8,128)(2,1)} %bitcast.69), calls=%async_computation.3 | async-start | bytes 786432 | tf_op jit(solution)/shard_map/all_to_all | solution.py:77
  164.9 11.6 %all-to-all-start.4 = ((f32[8,24,256]{2,1,0:T(8,128)}), f32[8,24,256]{2,1,0:T(8,128)S(1)}, u32[]{:S(2)}, u32[]{:S(2)}) async-start(f32[8,24,256]{2,1,0:T(8,128)} %broadcast_in_dim.39), calls=%async_computation.4 | async-start | bytes 393216 | tf_op jit(solution)/shard_map/all_to_all | solution.py:85
  176.5 0.7 copy-start.1

commit v3 on v2

--- a/solution.py
+++ b/solution.py
@@ -164,13 +164,14 @@
 ):
     local, channels, slices = energy_ref.shape
     unit = 2 * channels + 16
+    values = in_ref[...].astype(jnp.float32)
     div = []
     part = []
     for h in range(local):
         base = h * unit
-        div.append(in_ref[base : base + channels, :])
-        part.append(in_ref[base + channels : base + 2 * channels, :])
-        tail = in_ref[base + 2 * channels : base + unit, :]
+        div.append(values[base : base + channels, :])
+        part.append(values[base + channels : base + 2 * channels, :])
+        tail = values[base + 2 * channels : base + unit, :]
         tail = jnp.concatenate([tail[:, :128], tail[:, 128:]], axis=0)
         energy_ref[h] = tail[:, :slices]
         square = tail[:, slices : slices + channels]
@@ -179,9 +180,9 @@
     div_ref[...] = jnp.concatenate(div, axis=0)
     part_ref[...] = jnp.concatenate(part, axis=0)
     base = local * unit
-    scale_ref[...] = in_ref[base : base + 1, :]
-    premlp_ref[...] = in_ref[base + 1 : base + 2, :]
-    offset_ref[...] = in_ref[base + 2 : base + 3, :]
+    scale_ref[...] = values[base : base + 1, :]
+    premlp_ref[...] = values[base + 1 : base + 2, :]
+    offset_ref[...] = values[base + 2 : base + 3, :]
 
 
 def norm_kernel(member_ref, x_ref, gain_ref, s_ref):
@@ -712,7 +713,8 @@
     )
 
     head_grads, grads = lax.optimization_barrier((head_grads, grads))
-    head_grads = gather(exchange_sum(head_grads, everyone), ("pts",))
+    head_grads = exchange_sum(head_grads, everyone).astype(jnp.bfloat16)
+    head_grads = gather(head_grads, ("pts",))
     row = jax.ShapeDtypeStruct((1, width), jnp.float32)
     flat = jax.ShapeDtypeStruct((local * channels, width), jnp.float32)
     divider_slope, partition_slope, energy_slope, sharp_slope, scale_slope, premlp_slope, offset_slope = (

time: 180 us -> 178 us (0.989)
  waiting for transfers between devices: 48.1 us -> 46.1 us
  transfers between devices with their start and end apart: 19 -> 19, of which waited for: 13 -> 13; matrix products, arithmetic and copies ran while one was open for 5% -> 6% of each run, Pallas kernels for 16% -> 16%
where the time goes in v3:
time: 178 us; the launch traced here: 177 us
  Pallas kernels  74.5 us (42%)
  waiting for transfers between devices  46.1 us (26%)
  starting transfers between devices  36.8 us (21%)
  local copies, waits for them, and re-layouts  9.86 us (6%)
  matrix products  6.07 us (3%)
  other arithmetic  2.43 us (1%)
    pallas_call x1, Pallas kernels, body(): pl.pallas_call(functools.partial(mixer_kernel, heads=heads, slices=slices...  25.4 us
    pallas_call x1, Pallas kernels, body(): back_call(scaled, back_low, pair, token_emit, den_rows, moment, energy_ro...  22.4 us
    all_to_all x2, waiting for transfers between devices, exchange_sum(): lax.all_to_all(value.reshape(count, block, value.shape[1]), axes, 0, 0, t...  19.3 us
    ppermute x14, waiting for transfers between devices, swap(): return lax.ppermute(value, axis, [(i, i ^ distance) for i in range(size)])  17 us
    ppermute x14, starting transfers between devices, swap(): return lax.ppermute(value, axis, [(i, i ^ distance) for i in range(size)])  16.1 us
    pallas_call x1, Pallas kernels, body(): pl.pallas_call(functools.partial(front_kernel, heads=heads, slices=slices...  14 us
    all_to_all x2, starting transfers between devices, exchange_sum(): lax.all_to_all(value.reshape(count, block, value.shape[1]), axes, 0, 0, t...  9.35 us
    pallas_call x1, Pallas kernels, body(): pl.pallas_call(norm_kernel, grid_spec=pltpu.PrefetchScalarGridSpec(num_sc...  6.34 us
  transfers between devices with their start and end apart: 19, of which 13 were waited for; matrix products, arithmetic and copies ran while one was open for 6% of the time, Pallas kernels for 16%

profile of v3, /device:TPU:0, one launch (start us, length us, event | category | flops | bytes accessed | tf_op | source)
XLA Modules:
  0.0 176.7 jit_solution(9977119092048497139)
XLA Ops:
  0.6 1.9 %pack.1 = f32[4,192,256]{2,1,0:T(8,128)} custom-call(bf16[64,256]{1,0:T(8,128)(2,1)} %bitcast.72, bf16[64,256]{1,0:T(8,128)(2,1)} %bitcast.73, f32[1,64]{1,0:T(1,128)} %bitcast.74, f32[2,32,64]{2,1,0:T(8,128)} %energy_ref.1, f32[2,32,32]{2,1,0:T(8,128)} %ask_ref.1, f32[2,32,32]{2,1,0:T(8,128)} %look_ref.1, f32[2,32,32]{2,1,0:T(8,128)} %content_ref.1), custom_call_target="tpu_custom_call" | custom-call | tf_op jit(solution)/shard_map/pack/pallas_call | solution.py:510
  2.5 5.2 %all-to-all-start = ((f32[4,192,256]{2,1,0:T(8,128)}), f32[4,192,256]{2,1,0:T(8,128)S(1)}, u32[]{:S(2)}, u32[]{:S(2)}) async-start(f32[4,192,256]{2,1,0:T(8,128)} %pack.1), calls=%async_computation | async-start | bytes 1572864 | tf_op jit(solution)/shard_map/all_to_all | solution.py:523
  7.7 6.3 %norm.1.s_ref = bf16[8192,256]{1,0:T(8,128)(2,1)} custom-call(s32[1]{0:T(128)} %bitcast.member_ref, bf16[32768,256]{1,0:T(8,128)(2,1)} %x_ref.3, f32[1,256]{1,0:T(1,128)} %bitcast.79), custom_call_target="tpu_custom_call" | custom-call | flops 8589934592 | bytes 16777216 | tf_op jit(solution)/shard_map/norm/pallas_call | solution.py:546
  14.1 4.5 %all-to-all-done = f32[4,192,256]{2,1,0:T(8,128)S(1)} async-done(((f32[4,192,256]{2,1,0:T(8,128)}), f32[4,192,256]{2,1,0:T(8,128)S(1)}, u32[]{:S(2)}, u32[]{:S(2)}) %all-to-all-start) | async-done | bytes 786464 | tf_op jit(solution)/shard_map/all_to_all | solution.py:523
  18.6 0.9 copy-done
  19.4 2.7 %unpack.1 = (bf16[528,512]{1,0:T(8,128)(2,1)}, f32[256,528]{1,0:T(8,128)}, bf16[256,256]{1,0:T(8,128)(2,1)}, bf16[256,256]{1,0:T(8,128)(2,1)}, f32[8,32,32]{2,1,...) custom-call(f32[768,256]{1,0:T(8,128)} %bitcast.66), custom_call_target="tpu_custom_call" | custom-call | tf_op jit(solution)/shard_map/unpack/pallas_call | solution.py:526
  22.2 14.0 %front.1 = (bf16[512,8192]{1,0:T(8,128)(2,1)}, f32[512,256]{1,0:T(8,128)}, f32[40,512]{1,0:T(8,128)}) custom-call(bf16[8192,256]{1,0:T(8,128)(2,1)} %norm.1.s_ref, bf16[528,512]{1,0:T(8,128)(2,1)} %get-tuple-element.39.pair_ref, bf16[256,256]{1,0:T(8,128)(2,1)} %get-tuple-element.40.feat_ref.part_ref), custom_call_target="tpu_custom_call" | custom-call | flops 17179869184 | bytes 33554432 | tf_op jit(solution)/shard_map/front/pallas_call | solution.py:559
  36.2 1.5 collective-permute-done
  37.7 0.9 add.67
  38.6 1.7 collective-permute-start.1
  40.3 2.6 %collective-permute-start.2 = (f32[40,512]{1,0:T(8,128)S(1)}, f32[40,512]{1,0:T(8,128)S(1)}, u32[]{:S(2)}, u32[]{:S(2)}) collective-permute-start(f32[40,512]{1,0:T(8,128)S(1)} %add.67), channel_id=1, source_target_pairs={{0,16},{4,20},{8,24},{12,28},{16,0},{20,4},{24,8},{28,12},{1,17},{... | collective-permute-start | bytes 245768 | tf_op jit(solution)/shard_map/ppermute | solution.py:52
  43.1 0.8 copy.40
  43.8 0.8 copy.41
  44.6 5.2 %collective-permute-done.2 = f32[40,512]{1,0:T(8,128)S(1)} collective-permute-done((f32[40,512]{1,0:T(8,128)S(1)}, f32[40,512]{1,0:T(8,128)S(1)}, u32[]{:S(2)}, u32[]{:S(2)}) %collective-permute-start.2) | collective-permute-done | bytes 81952 | tf_op jit(solution)/shard_map/ppermute | solution.py:52
  49.8 1.5 collective-permute-start.4
  51.3 0.6 collective-permute-start.5
  51.8 1.5 collective-permute-start.6
  53.3 1.2 collective-permute-done.4
  54.6 1.1 collective-permute-done.5
  55.7 1.5 collective-permute-done.6
  57.4 0.4 fusion.20
  57.8 0.4 fusion.21
  58.2 0.4 fusion.22
  58.6 0.6 fusion.2
  59.2 0.4 convolution_convert_fusion
  59.7 1.0 mul.100.token_ref
  60.8 25.4 %mixer.1 = (bf16[8192,256]{1,0:T(8,128)(2,1)}, bf16[8192,256]{1,0:T(8,128)(2,1)}, bf16[768,256]{1,0:T(8,128)(2,1)}, f32[8,256]{1,0:T(8,128)}, f32[32,512]{1,0:T(8,128)}, /*index=5*/bf16[512,256]{1,0:T(8,128)(2,1)}) custom-call(s32[1]{0:T(128)} %bitcast.member_ref, bf16[32768,256]{1,0:T(8,128)(2,1)} %x_ref.3, bf16[512,8192]{1,0:T(8,128)(2,1)} %get-tuple-element.41.w_ref, ...), custom_call_target="tpu_custom_call" | custom-call | flops 27917287424 | bytes 54525952 | tf_op jit(solution)/shard_map/mixer/pallas_call | solution.py:596
  86.3 1.5 collective-permute-done.7
  87.7 0.8 add.77
  88.6 2.6 %collective-permute-start.10 = (f32[32,512]{1,0:T(8,128)S(1)}, f32[32,512]{1,0:T(8,128)S(1)}, u32[]{:S(2)}, u32[]{:S(2)}) collective-permute-start(f32[32,512]{1,0:T(8,128)S(1)} %add.77), channel_id=1, source_target_pairs={{0,24},{4,28},{8,16},{12,20},{16,8},{20,12},{24,0},{28,4},{1,25},{... | collective-permute-start | bytes 196616 | tf_op jit(solution)/shard_map/ppermute | solution.py:52
  91.2 0.5 collective-permute-start.8
  91.7 1.3 collective-permute-start.9
  93.0 2.3 %collective-permute-done.10 = f32[32,512]{1,0:T(8,128)S(1)} collective-permute-done((f32[32,512]{1,0:T(8,128)S(1)}, f32[32,512]{1,0:T(8,128)S(1)}, u32[]{:S(2)}, u32[]{:S(2)}) %collective-permute-start.10) | collective-permute-done | bytes 65568 | tf_op jit(solution)/shard_map/ppermute | solution.py:52
  95.3 1.9 %collective-permute-done.8 = f32[32,512]{1,0:T(8,128)S(1)} collective-permute-done((f32[32,512]{1,0:T(8,128)S(1)}, f32[32,512]{1,0:T(8,128)S(1)}, u32[]{:S(2)}, u32[]{:S(2)}) %collective-permute-start.8) | collective-permute-done | bytes 65568 | tf_op jit(solution)/shard_map/ppermute | solution.py:52
  97.2 0.9 collective-permute-done.9
  98.1 1.6 collective-permute-start.11
  99.7 0.6 collective-permute-start.12
  100.3 1.4 collective-permute-start.13
  101.7 3.7 %all-to-all-start.1 = ((bf16[32,24,256]{2,1,0:T(8,128)(2,1)}), bf16[32,24,256]{2,1,0:T(8,128)(2,1)S(1)}, u32[]{:S(2)}, u32[]{:S(2)}) async-start(bf16[32,24,256]{2,1,0:T(8,128)(2,1)} %bitcast.67), calls=%async_computation.1 | async-start | bytes 786432 | tf_op jit(solution)/shard_map/all_to_all | solution.py:77
  105.6 0.5 fusion.5
  106.1 0.6 multiply_reduce_fusion
  106.9 0.5 fusion.25
  107.4 0.4 fusion.26
  108.0 0.3 convolution_add_fusion.1
  108.3 0.3 fusion.12
  108.7 1.0 mul.116.num_ref
  109.7 0.9 neg.24.den_ref
  110.7 8.2 %all-to-all-done.1 = bf16[32,24,256]{2,1,0:T(8,128)(2,1)S(1)} async-done(((bf16[32,24,256]{2,1,0:T(8,128)(2,1)}), bf16[32,24,256]{2,1,0:T(8,128)(2,1)S(1)}, u32[]{:S(2)}, u32[]{:S(2)}) %all-to-all-start.1) | async-done | bytes 393248 | tf_op jit(solution)/shard_map/all_to_all | solution.py:77
  118.9 0.8 broadcast_in_dim.38
  119.7 2.8 %all-to-all-start.2 = ((bf16[32,24,256]{2,1,0:T(8,128)(2,1)}), bf16[32,24,256]{2,1,0:T(8,128)(2,1)S(1)}, u32[]{:S(2)}, u32[]{:S(2)}) async-start(bf16[32,24,256]{2,1,0:T(8,128)(2,1)} %broadcast_in_dim.38), calls=%async_computation.2 | async-start | bytes 786432 | tf_op jit(solution)/shard_map/all_to_all | solution.py:85
  122.5 22.4 %back.1 = bf16[768,256]{1,0:T(8,128)(2,1)} custom-call(bf16[8192,256]{1,0:T(8,128)(2,1)} %norm.1.s_ref, bf16[8192,256]{1,0:T(8,128)(2,1)} %get-tuple-element.47.back_ref, bf16[528,512]{1,0:T(8,128)(2,1)} %get-tuple-element.39.pair_ref, bf16[512,256]{1,0:T(8,128)(2,1)} %get-tuple-element.48.te_ref, f32[512,1]{1,0:T(8,128)} %neg.24.den_ref, ...), custom_call_target="tpu_custom_call" | custom-call | flops 27917287424 | bytes 54525952 | tf_op jit(solution)/shard_map/back/pallas_call | solution.py:700
  145.0 5.6 %all-to-all-start.3 = ((bf16[32,24,256]{2,1,0:T(8,128)(2,1)}), bf16[32,24,256]{2,1,0:T(8,128)(2,1)S(1)}, u32[]{:S(2)}, u32[]{:S(2)}) async-start(bf16[32,24,256]{2,1,0:T(8,128)(2,1)} %bitcast.68), calls=%async_computation.3 | async-start | bytes 786432 | tf_op jit(solution)/shard_map/all_to_all | solution.py:77
  150.7 0.3 fusion.19
  151.0 0.6 constant_dynamic-slice_fusion.2
  151.7 0.3 fusion.18
  152.0 0.3 fusion.17
  152.3 0.6 constant_dynamic-slice_fusion
  153.0 11.1 %all-to-all-done.3 = bf16[32,24,256]{2,1,0:T(8,128)(2,1)S(1)} async-done(((bf16[32,24,256]{2,1,0:T(8,128)(2,1)}), bf16[32,24,256]{2,1,0:T(8,128)(2,1)S(1)}, u32[]{:S(2)}, u32[]{:S(2)}) %all-to-all-start.3) | async-done | bytes 393248 | tf_op jit(solution)/shard_map/all_to_all | solution.py:77
  164.2 0.7 broadcast_in_dim.39
  164.8 3.4 %all-to-all-start.4 = ((bf16[8,24,256]{2,1,0:T(8,128)(2,1)}), bf16[8,24,256]{2,1,0:T(8,128)(2,1)S(1)}, u32[]{:S(2)}, u32[]{:S(2)}) async-start(bf16[8,24,256]{2,1,0:T(8,128)(2,1)} %broadcast_in_dim.39), calls=%async_computation.4 | async-start | bytes 196608 | tf_op jit(solution)/shard_map/all_to_all | solution.py:85
  168.2 0.9 fusion.23
  169.1 5.4 %all-to-all-done.4 = bf16[8,24,256]{2,1,0:T(8,128)(2,1)S(1)} async-done(((bf16[8,24,256]{2,1,0:T(8,128)(2,1)}), bf16[8,24,256]{2,1,0:T(8,128)(2,1)S(1)}, u32[]{:S(2)}, u32[]{:S(2)}) %all-to-all-start.4) | async-done | bytes 98336 | tf_op jit(solution)/shard_map/all_to_all | solution.py:85
  174.4 0.6 copy-done.1
  175.1 1.6 finish.1
  (42 shorter events, 1.5 us)
Async XLA Ops:
  2.5 16.0 %all-to-all-start = ((f32[4,192,256]{2,1,0:T(8,128)}), f32[4,192,256]{2,1,0:T(8,128)S(1)}, u32[]{:S(2)}, u32[]{:S(2)}) async-start(f32[4,192,256]{2,1,0:T(8,128)} %pack.1), calls=%async_computation | async-start | bytes 1572864 | tf_op jit(solution)/shard_map/all_to_all | solution.py:523
  18.6 0.9 copy-start
  22.1 20.9 %copy-start.3 = (bf16[256,256]{1,0:T(8,128)(2,1)S(1)}, bf16[256,256]{1,0:T(8,128)(2,1)}, u32[]{:S(2)}) copy-start(bf16[256,256]{1,0:T(8,128)(2,1)} %expand_ref.1) | copy-start | bytes 393220
  22.1 21.7 %copy-start.4 = (bf16[256,256]{1,0:T(8,128)(2,1)S(1)}, bf16[256,256]{1,0:T(8,128)(2,1)}, u32[]{:S(2)}) copy-start(bf16[256,256]{1,0:T(8,128)(2,1)} %contract_ref.1) | copy-start | bytes 393220
  22.1 35.2 %copy-start.5 = (f32[8,32,32]{2,1,0:T(8,128)S(1)}, f32[8,32,32]{2,1,0:T(8,128)}, u32[]{:S(2)}) copy-start(f32[8,32,32]{2,1,0:T(8,128)} %get-tuple-element.45) | copy-start | bytes 98308
  22.2 35.6 %copy-start.6 = (f32[8,32,32]{2,1,0:T(8,128)S(1)}, f32[8,32,32]{2,1,0:T(8,128)}, u32[]{:S(2)}) copy-start(f32[8,32,32]{2,1,0:T(8,128)} %get-tuple-element.44) | copy-start | bytes 98308
  22.2 36.0 %copy-start.2 = (f32[8,32,32]{2,1,0:T(8,128)S(1)}, f32[8,32,32]{2,1,0:T(8,128)}, u32[]{:S(2)}) copy-start(f32[8,32,32]{2,1,0:T(8,128)} %get-tuple-element.43) | copy-start | bytes 98308
  36.2 1.5 collective-permute-start
  38.6 6.0 %collective-permute-start.1 = (f32[40,512]{1,0:T(8,128)S(1)}, f32[40,512]{1,0:T(8,128)S(1)}, u32[]{:S(2)}, u32[]{:S(2)}) collective-permute-start(f32[40,512]{1,0:T(8,128)S(1)} %add.67), channel_id=1, source_target_pairs={{0,8},{4,12},{8,0},{12,4},{16,24},{20,28},{24,16},{28,20},{1,9},{5... | collective-permute-start | bytes 245768 | tf_op jit(solution)/shard_map/ppermute | solution.py:52
  40.3 9.5 %collective-permute-start.2 = (f32[40,512]{1,0:T(8,128)S(1)}, f32[40,512]{1,0:T(8,128)S(1)}, u32[]{:S(2)}, u32[]{:S(2)}) collective-permute-start(f32[40,512]{1,0:T(8,128)S(1)} %add.67), channel_id=1, source_target_pairs={{0,16},{4,20},{8,24},{12,28},{16,0},{20,4},{24,8},{28,12},{1,17},{... | collective-permute-start | bytes 245768 | tf_op jit(solution)/shard_map/ppermute | solution.py:52
  42.9 6.9 %collective-permute-start.3 = (f32[40,512]{1,0:T(8,128)S(1)}, f32[40,512]{1,0:T(8,128)S(1)}, u32[]{:S(2)}, u32[]{:S(2)}) collective-permute-start(f32[40,512]{1,0:T(8,128)S(1)} %add.67), channel_id=1, source_target_pairs={{0,24},{4,28},{8,16},{12,20},{16,8},{20,12},{24,0},{28,4},{1,25},{... | collective-permute-start | bytes 245768 | tf_op jit(solution)/shard_map/ppermute | solution.py:52
  49.8 4.8 %collective-permute-start.4 = (f32[40,512]{1,0:T(8,128)S(1)}, f32[40,512]{1,0:T(8,128)S(1)}, u32[]{:S(2)}, u32[]{:S(2)}) collective-permute-start(f32[40,512]{1,0:T(8,128)S(1)} %add_add_fusion.1), channel_id=1, source_target_pairs={{0,1},{1,0},{2,3},{3,2},{4,5},{5,4},{6,7},{7,6},{8,9},{9,8},{10,11... | collective-permute-start | bytes 245768 | tf_op jit(solution)/shard_map/ppermute | solution.py:52
  51.3 4.4 %collective-permute-start.5 = (f32[40,512]{1,0:T(8,128)S(1)}, f32[40,512]{1,0:T(8,128)S(1)}, u32[]{:S(2)}, u32[]{:S(2)}) collective-permute-start(f32[40,512]{1,0:T(8,128)S(1)} %add_add_fusion.1), channel_id=1, source_target_pairs={{0,2},{1,3},{2,0},{3,1},{4,6},{5,7},{6,4},{7,5},{8,10},{9,11},{10,... | collective-permute-start | bytes 245768 | tf_op jit(solution)/shard_map/ppermute | solution.py:52
  51.8 5.3 %collective-permute-start.6 = (f32[40,512]{1,0:T(8,128)S(1)}, f32[40,512]{1,0:T(8,128)S(1)}, u32[]{:S(2)}, u32[]{:S(2)}) collective-permute-start(f32[40,512]{1,0:T(8,128)S(1)} %add_add_fusion.1), channel_id=1, source_target_pairs={{0,3},{1,2},{2,1},{3,0},{4,7},{5,6},{6,5},{7,4},{8,11},{9,10},{10,... | collective-permute-start | bytes 245768 | tf_op jit(solution)/shard_map/ppermute | solution.py:52
  86.2 1.5 collective-permute-start.7
  88.6 6.7 %collective-permute-start.10 = (f32[32,512]{1,0:T(8,128)S(1)}, f32[32,512]{1,0:T(8,128)S(1)}, u32[]{:S(2)}, u32[]{:S(2)}) collective-permute-start(f32[32,512]{1,0:T(8,128)S(1)} %add.77), channel_id=1, source_target_pairs={{0,24},{4,28},{8,16},{12,20},{16,8},{20,12},{24,0},{28,4},{1,25},{... | collective-permute-start | bytes 196616 | tf_op jit(solution)/shard_map/ppermute | solution.py:52
  91.2 6.0 %collective-permute-start.8 = (f32[32,512]{1,0:T(8,128)S(1)}, f32[32,512]{1,0:T(8,128)S(1)}, u32[]{:S(2)}, u32[]{:S(2)}) collective-permute-start(f32[32,512]{1,0:T(8,128)S(1)} %add.77), channel_id=1, source_target_pairs={{0,8},{4,12},{8,0},{12,4},{16,24},{20,28},{24,16},{28,20},{1,9},{5... | collective-permute-start | bytes 196616 | tf_op jit(solution)/shard_map/ppermute | solution.py:52
  91.7 6.4 %collective-permute-start.9 = (f32[32,512]{1,0:T(8,128)S(1)}, f32[32,512]{1,0:T(8,128)S(1)}, u32[]{:S(2)}, u32[]{:S(2)}) collective-permute-start(f32[32,512]{1,0:T(8,128)S(1)} %add.77), channel_id=1, source_target_pairs={{0,16},{4,20},{8,24},{12,28},{16,0},{20,4},{24,8},{28,12},{1,17},{... | collective-permute-start | bytes 196616 | tf_op jit(solution)/shard_map/ppermute | solution.py:52
  98.1 7.3 %collective-permute-start.11 = (f32[32,512]{1,0:T(8,128)S(1)}, f32[32,512]{1,0:T(8,128)S(1)}, u32[]{:S(2)}, u32[]{:S(2)}) collective-permute-start(f32[32,512]{1,0:T(8,128)S(1)} %add_add_fusion.3), channel_id=1, source_target_pairs={{0,1},{1,0},{2,3},{3,2},{4,5},{5,4},{6,7},{7,6},{8,9},{9,8},{10,11... | collective-permute-start | bytes 196616 | tf_op jit(solution)/shard_map/ppermute | solution.py:52
  99.7 5.7 %collective-permute-start.12 = (f32[32,512]{1,0:T(8,128)S(1)}, f32[32,512]{1,0:T(8,128)S(1)}, u32[]{:S(2)}, u32[]{:S(2)}) collective-permute-start(f32[32,512]{1,0:T(8,128)S(1)} %add_add_fusion.3), channel_id=1, source_target_pairs={{0,2},{1,3},{2,0},{3,1},{4,6},{5,7},{6,4},{7,5},{8,10},{9,11},{10,... | collective-permute-start | bytes 196616 | tf_op jit(solution)/shard_map/ppermute | solution.py:52
  100.3 5.2 %collective-permute-start.13 = (f32[32,512]{1,0:T(8,128)S(1)}, f32[32,512]{1,0:T(8,128)S(1)}, u32[]{:S(2)}, u32[]{:S(2)}) collective-permute-start(f32[32,512]{1,0:T(8,128)S(1)} %add_add_fusion.3), channel_id=1, source_target_pairs={{0,3},{1,2},{2,1},{3,0},{4,7},{5,6},{6,5},{7,4},{8,11},{9,10},{10,... | collective-permute-start | bytes 196616 | tf_op jit(solution)/shard_map/ppermute | solution.py:52
  101.7 17.2 %all-to-all-start.1 = ((bf16[32,24,256]{2,1,0:T(8,128)(2,1)}), bf16[32,24,256]{2,1,0:T(8,128)(2,1)S(1)}, u32[]{:S(2)}, u32[]{:S(2)}) async-start(bf16[32,24,256]{2,1,0:T(8,128)(2,1)} %bitcast.67), calls=%async_computation.1 | async-start | bytes 786432 | tf_op jit(solution)/shard_map/all_to_all | solution.py:77
  119.7 25.3 %all-to-all-start.2 = ((bf16[32,24,256]{2,1,0:T(8,128)(2,1)}), bf16[32,24,256]{2,1,0:T(8,128)(2,1)S(1)}, u32[]{:S(2)}, u32[]{:S(2)}) async-start(bf16[32,24,256]{2,1,0:T(8,128)(2,1)} %broadcast_in_dim.38), calls=%async_computation.2 | async-start | bytes 786432 | tf_op jit(solution)/shard_map/all_to_all | solution.py:85
  145.0 19.1 %all-to-all-start.3 = ((bf16[32,24,256]{2,1,0:T(8,128)(2,1)}), bf16[32,24,256]{2,1,0:T(8,128)(2,1)S(1)}, u32[]{:S(2)}, u32[]{:S(2)}) async-start(bf16[32,24,256]{2,1,0:T(8,128)(2,1)} %bitcast.68), calls=%async_computation.3 | async-start | bytes 786432 | tf_op jit(solution)/shard_map/all_to_all | solution.py:77
  164.8 9.6 %all-to-all-start.4 = ((bf16[8,24,256]{2,1,0:T(8,128)(2,1)}), bf16[8,24,256]{2,1,0:T(8,128)(2,1)S(1)}, u32[]{:S(2)}, u32[]{:S(2)}) async-start(bf16[8,24,256]{2,1,0:T(8,128)(2,1)} %broadcast_in_dim.39), calls=%async_computation.4 | async-start | bytes 196608 | tf_op jit(solution)/shard_map/all_to_all | solution.py:85
  174.4 0.6 copy-start.1
